TPU v7x, 32 devices: a whole 2x2x4 slice. The times are simulated.
32 devices in a mesh: shard: 16 (over z, x, core), rep: 2 (over y).
Axes of the slice: x: 2, y: 2, z: 4, core: 2. Of those that a mesh axis runs over, the one named last changes fastest.
Arguments:
- hidden_in: bfloat16 [2, 32, 128, 1024], P(None, ('shard', 'rep')), may hold values from -6 to 6
- encoded: bfloat16 [2, 32, 256, 1024], P(None, ('shard', 'rep')), may hold values from -6 to 6
- dec_segments: int32 [2, 32, 128], P(None, ('shard', 'rep')), may hold values from 0 to 2, never falling along the last dimension, each value on 1 to 64 neighbouring positions
- enc_segments: int32 [2, 32, 256], P(None, ('shard', 'rep')), may hold values from 0 to 2, never falling along the last dimension, each value on 1 to 128 neighbouring positions
- buckets: int32 [128], replicated, may hold values from 0 to 31
- out_cot: bfloat16 [2, 32, 128, 1024], P(None, ('shard', 'rep')), may hold values from -6 to 6
- norm_self: bfloat16 [1024], P('shard'), may hold values from 0.5 to 1.5
- self_query: bfloat16 [1024, 1024], P('shard'), may hold values from -0.0234375 to 0.0234375
- self_key: bfloat16 [1024, 1024], P('shard'), may hold values from -0.1875 to 0.1875
- self_value: bfloat16 [1024, 1024], P('shard'), may hold values from -0.1875 to 0.1875
- self_out: bfloat16 [1024, 1024], P('shard'), may hold values from -1.5 to 1.5
- relative_bias_table: bfloat16 [32, 16], replicated, may hold values from -4 to 4
- norm_cross: bfloat16 [1024], P('shard'), may hold values from 0.5 to 1.5
- cross_query: bfloat16 [1024, 1024], P('shard'), may hold values from -0.0234375 to 0.0234375
- cross_key: bfloat16 [1024, 1024], P('shard'), may hold values from -0.1875 to 0.1875
- cross_value: bfloat16 [1024, 1024], P('shard'), may hold values from -0.1875 to 0.1875
- cross_out: bfloat16 [1024, 1024], P('shard'), may hold values from -1.5 to 1.5
- norm_ff: bfloat16 [1024], P('shard'), may hold values from 0.5 to 1.5
- ff_gate: bfloat16 [1024, 2816], P('shard'), may hold values from -0.1875 to 0.1875
- ff_up: bfloat16 [1024, 2816], P('shard'), may hold values from -0.1875 to 0.1875
- ff_down: bfloat16 [2816, 1024], P('shard'), may hold values from -0.21875 to 0.21875
Outputs:
- out_hidden: bfloat16 [2, 32, 128, 1024], P(None, ('shard', 'rep'))
- grad_hidden: float32 [2, 32, 128, 1024], P(None, ('shard', 'rep'))
- grad_encoded: float32 [2, 32, 256, 1024], P(None, ('shard', 'rep'))
- grad_norm_self: float32 [1024], P('shard')
- grad_self_query: float32 [1024, 1024], P('shard')
- grad_self_key: float32 [1024, 1024], P('shard')
- grad_self_value: float32 [1024, 1024], P('shard')
- grad_self_out: float32 [1024, 1024], P('shard')
- grad_rel_table: float32 [32, 16], replicated
- grad_norm_cross: float32 [1024], P('shard')
- grad_cross_query: float32 [1024, 1024], P('shard')
- grad_cross_key: float32 [1024, 1024], P('shard')
- grad_cross_value: float32 [1024, 1024], P('shard')
- grad_cross_out: float32 [1024, 1024], P('shard')
- grad_norm_ff: float32 [1024], P('shard')
- grad_ff_gate: float32 [1024, 2816], P('shard')
- grad_ff_up: float32 [1024, 2816], P('shard')
- grad_ff_down: float32 [2816, 1024], P('shard')
Inputs may be any that keep to these rules, and one draw needn't show every extreme that they name: `dec_segments`: within a sequence the decoder document numbers never fall; each of the 3 documents holds one or more positions, the longest exactly half of 128. `enc_segments`: within a sequence the encoder document numbers never fall; each of the 3 documents holds one or more positions, the longest exactly half of 256.
All inputs are finite; a program needn't handle non-finite values.
Results may differ from a plain program's by a relative error of at most 0.019.
Values may be sent and summed in bfloat16 or wider, within the bound.
A program may use at most 192 MiB of HBM per device.

v0:
```python
import jax
import jax.numpy as jnp
from jax import lax
from jax.sharding import PartitionSpec as P

HEADS = 16
HEAD = 64


EPS = 1e-06
NEG = -1e30


def matmul(left, right):
    return jnp.dot(left, right, preferred_element_type=jnp.float32)


def outer_sum(left, right):
    return lax.dot_general(
        left, right, (((0,), (0,)), ((), ())), preferred_element_type=jnp.float32
    )


def back_mul(left, right):
    return lax.dot_general(
        left, right, (((1,), (1,)), ((), ())), preferred_element_type=jnp.float32
    )


def rms_norm(values, gain):
    return values * lax.rsqrt(jnp.mean(values * values, axis=-1, keepdims=True) + EPS) * gain


def gated(gate, upper):
    return jax.nn.gelu(gate, approximate=True) * upper


def split_heads(values):
    return values.reshape(values.shape[0], HEADS, HEAD)


def raw_scores(query, keys, position_bias, allowed):
    scores = (
        jnp.einsum(
            "qhd,khd->hqk",
            split_heads(query),
            split_heads(keys),
            preferred_element_type=jnp.float32,
        )
        + position_bias
    )
    return jnp.where(allowed[None], scores, NEG)


def attend_forward(query, keys, values, position_bias, allowed):
    scores = raw_scores(query, keys, position_bias, allowed)
    top = jnp.max(scores, axis=-1, keepdims=True)
    expo = jnp.exp(scores - top)
    total = jnp.sum(expo, axis=-1, keepdims=True)
    probs = (expo / total).astype(jnp.bfloat16)
    mixed = jnp.einsum(
        "hqk,khd->qhd", probs, split_heads(values), preferred_element_type=jnp.float32
    )
    return (mixed.reshape(query.shape[0], -1).astype(jnp.bfloat16), top + jnp.log(total))


def attend_backward(query, keys, values, position_bias, allowed, logsum, grad_mixed):
    scores = raw_scores(query, keys, position_bias, allowed)
    probs = jnp.exp(scores - logsum)
    grad_probs = jnp.einsum(
        "qhd,khd->hqk",
        split_heads(grad_mixed),
        split_heads(values),
        preferred_element_type=jnp.float32,
    )
    score_gradient_rows = (
        probs * (grad_probs - jnp.sum(probs * grad_probs, axis=-1, keepdims=True))
    ).astype(jnp.bfloat16)
    rows = query.shape[0]
    cols = keys.shape[0]
    grad_query = jnp.einsum(
        "hqk,khd->qhd", score_gradient_rows, split_heads(keys), preferred_element_type=jnp.float32
    )
    grad_keys = jnp.einsum(
        "hqk,qhd->khd", score_gradient_rows, split_heads(query), preferred_element_type=jnp.float32
    )
    grad_values = jnp.einsum(
        "hqk,qhd->khd",
        probs.astype(jnp.bfloat16),
        split_heads(grad_mixed),
        preferred_element_type=jnp.float32,
    )
    return (
        grad_query.reshape(rows, -1).astype(jnp.bfloat16),
        grad_keys.reshape(cols, -1).astype(jnp.bfloat16),
        grad_values.reshape(cols, -1).astype(jnp.bfloat16),
        score_gradient_rows,
    )


def layer_pass(
    tokens, encoded, dec_seg, enc_seg, cot, attention_weights, bucket_indicator, position_bias
):
    (
        gain_self,
        w_query,
        w_key,
        w_value,
        w_out,
        gain_cross,
        c_query,
        c_key,
        c_value,
        c_out,
        gain_ff,
        w_gate,
        w_up,
        w_down,
    ) = attention_weights
    spots = jnp.arange(tokens.shape[0])
    self_mask = (spots[:, None] >= spots[None, :]) & (dec_seg[:, None] == dec_seg[None, :])
    cross_mask = dec_seg[:, None] == enc_seg[None, :]
    gain_one = gain_self.astype(jnp.float32)
    gain_two = gain_cross.astype(jnp.float32)
    gain_three = gain_ff.astype(jnp.float32)
    start = tokens.astype(jnp.float32)
    first = rms_norm(start, gain_one).astype(jnp.bfloat16)
    query = matmul(first, w_query).astype(jnp.bfloat16)
    keys = matmul(first, w_key).astype(jnp.bfloat16)
    values = matmul(first, w_value).astype(jnp.bfloat16)
    mixed, logsum = attend_forward(query, keys, values, position_bias, self_mask)
    middle = start + matmul(mixed, w_out)
    second = rms_norm(middle, gain_two).astype(jnp.bfloat16)
    cquery = matmul(second, c_query).astype(jnp.bfloat16)
    ckeys = matmul(encoded, c_key).astype(jnp.bfloat16)
    cvalues = matmul(encoded, c_value).astype(jnp.bfloat16)
    cmixed, clogsum = attend_forward(cquery, ckeys, cvalues, 0.0, cross_mask)
    late = middle + matmul(cmixed, c_out)
    third = rms_norm(late, gain_three).astype(jnp.bfloat16)
    gate = matmul(third, w_gate)
    upper = matmul(third, w_up)
    hidden = gated(gate, upper).astype(jnp.bfloat16)
    result = (late + matmul(hidden, w_down)).astype(jnp.bfloat16)
    grad_late = cot.astype(jnp.float32)
    branch_grad = grad_late.astype(jnp.bfloat16)
    down_wgrad = outer_sum(hidden, branch_grad)
    grad_hidden = back_mul(branch_grad, w_down)
    unused, pull = jax.vjp(gated, gate, upper)
    grad_gate, grad_upper = pull(grad_hidden)
    grad_gate = grad_gate.astype(jnp.bfloat16)
    grad_upper = grad_upper.astype(jnp.bfloat16)
    gate_wgrad = outer_sum(third, grad_gate)
    upper_wgrad = outer_sum(third, grad_upper)
    grad_third = back_mul(grad_gate, w_gate) + back_mul(grad_upper, w_up)
    unused, pull = jax.vjp(rms_norm, late, gain_three)
    grad_norm, gain3_grad = pull(grad_third)
    grad_middle = grad_late + grad_norm
    branch_grad = grad_middle.astype(jnp.bfloat16)
    cout_wgrad = outer_sum(cmixed, branch_grad)
    grad_cmixed = back_mul(branch_grad, c_out).astype(jnp.bfloat16)
    grad_cquery, grad_ckeys, grad_cvalues, unused = attend_backward(
        cquery, ckeys, cvalues, 0.0, cross_mask, clogsum, grad_cmixed
    )
    cquery_wgrad = outer_sum(second, grad_cquery)
    ckey_wgrad = outer_sum(encoded, grad_ckeys)
    cvalue_wgrad = outer_sum(encoded, grad_cvalues)
    grad_second = back_mul(grad_cquery, c_query)
    grad_encoded = back_mul(grad_ckeys, c_key) + back_mul(grad_cvalues, c_value)
    unused, pull = jax.vjp(rms_norm, middle, gain_two)
    grad_norm, gain2_grad = pull(grad_second)
    grad_start = grad_middle + grad_norm
    branch_grad = grad_start.astype(jnp.bfloat16)
    out_wgrad = outer_sum(mixed, branch_grad)
    grad_mixed = back_mul(branch_grad, w_out).astype(jnp.bfloat16)
    grad_query, grad_keys, grad_values, score_gradient_rows = attend_backward(
        query, keys, values, position_bias, self_mask, logsum, grad_mixed
    )
    bias_table_gradient = jnp.einsum(
        "xzc,wzc->wx", score_gradient_rows, bucket_indicator, preferred_element_type=jnp.float32
    )
    query_wgrad = outer_sum(first, grad_query)
    key_wgrad = outer_sum(first, grad_keys)
    value_wgrad = outer_sum(first, grad_values)
    grad_first = (
        back_mul(grad_query, w_query) + back_mul(grad_keys, w_key) + back_mul(grad_values, w_value)
    )
    unused, pull = jax.vjp(rms_norm, start, gain_one)
    grad_norm, gain1_grad = pull(grad_first)
    grad_tokens = grad_start + grad_norm
    grads = (
        gain1_grad,
        query_wgrad,
        key_wgrad,
        value_wgrad,
        out_wgrad,
        gain2_grad,
        cquery_wgrad,
        ckey_wgrad,
        cvalue_wgrad,
        cout_wgrad,
        gain3_grad,
        gate_wgrad,
        upper_wgrad,
        down_wgrad,
    )
    return (result, grad_tokens, grad_encoded, grads, bias_table_gradient)


def body(
    hidden_in,
    encoded,
    dec_segments,
    enc_segments,
    buckets,
    out_cot,
    norm_self,
    self_query,
    self_key,
    self_value,
    self_out,
    relative_bias_table,
    norm_cross,
    cross_query,
    cross_key,
    cross_value,
    cross_out,
    norm_ff,
    ff_gate,
    ff_up,
    ff_down,
):
    length = hidden_in.shape[2]
    spots = jnp.arange(length)
    distance = jnp.maximum(spots[:, None] - spots[None, :], 0)
    pair_bucket = jnp.take(buckets, distance)
    bucket_indicator = (
        pair_bucket[None] == jnp.arange(relative_bias_table.shape[0])[:, None, None]
    ).astype(jnp.bfloat16)
    position_bias = jnp.einsum(
        "mit,mn->nit", bucket_indicator, relative_bias_table, preferred_element_type=jnp.float32
    )
    micro = hidden_in.shape[0]
    totals = None
    table_total = jnp.zeros(relative_bias_table.shape, jnp.float32)
    results = []
    token_gradient_rows = []
    encoder_grads = []
    for step in range(micro):
        attention_weights = (
            lax.all_gather(norm_self, "shard", axis=0, tiled=True),
            lax.all_gather(self_query, "shard", axis=0, tiled=True),
            lax.all_gather(self_key, "shard", axis=0, tiled=True),
            lax.all_gather(self_value, "shard", axis=0, tiled=True),
            lax.all_gather(self_out, "shard", axis=0, tiled=True),
            lax.all_gather(norm_cross, "shard", axis=0, tiled=True),
            lax.all_gather(cross_query, "shard", axis=0, tiled=True),
            lax.all_gather(cross_key, "shard", axis=0, tiled=True),
            lax.all_gather(cross_value, "shard", axis=0, tiled=True),
            lax.all_gather(cross_out, "shard", axis=0, tiled=True),
            lax.all_gather(norm_ff, "shard", axis=0, tiled=True),
            lax.all_gather(ff_gate, "shard", axis=0, tiled=True),
            lax.all_gather(ff_up, "shard", axis=0, tiled=True),
            lax.all_gather(ff_down, "shard", axis=0, tiled=True),
        )
        result, grad_tokens, grad_enc, grads, bias_table_gradient = layer_pass(
            hidden_in[step, 0],
            encoded[step, 0],
            dec_segments[step, 0],
            enc_segments[step, 0],
            out_cot[step, 0],
            attention_weights,
            bucket_indicator,
            position_bias,
        )
        if totals is None:
            totals = tuple(grads)
        else:
            totals = tuple((acc + grad for acc, grad in zip(totals, grads)))
        table_total = table_total + bias_table_gradient
        results.append(result)
        token_gradient_rows.append(grad_tokens)
        encoder_grads.append(grad_enc)
    totals = (
        lax.psum_scatter(totals[0], "shard", scatter_dimension=0, tiled=True),
        lax.psum_scatter(totals[1], "shard", scatter_dimension=0, tiled=True),
        lax.psum_scatter(totals[2], "shard", scatter_dimension=0, tiled=True),
        lax.psum_scatter(totals[3], "shard", scatter_dimension=0, tiled=True),
        lax.psum_scatter(totals[4], "shard", scatter_dimension=0, tiled=True),
        lax.psum_scatter(totals[5], "shard", scatter_dimension=0, tiled=True),
        lax.psum_scatter(totals[6], "shard", scatter_dimension=0, tiled=True),
        lax.psum_scatter(totals[7], "shard", scatter_dimension=0, tiled=True),
        lax.psum_scatter(totals[8], "shard", scatter_dimension=0, tiled=True),
        lax.psum_scatter(totals[9], "shard", scatter_dimension=0, tiled=True),
        lax.psum_scatter(totals[10], "shard", scatter_dimension=0, tiled=True),
        lax.psum_scatter(totals[11], "shard", scatter_dimension=0, tiled=True),
        lax.psum_scatter(totals[12], "shard", scatter_dimension=0, tiled=True),
        lax.psum_scatter(totals[13], "shard", scatter_dimension=0, tiled=True),
    )
    totals = (
        lax.psum(totals[0].astype(jnp.bfloat16), "rep").astype(jnp.float32),
        lax.psum(totals[1].astype(jnp.bfloat16), "rep").astype(jnp.float32),
        lax.psum(totals[2].astype(jnp.bfloat16), "rep").astype(jnp.float32),
        lax.psum(totals[3].astype(jnp.bfloat16), "rep").astype(jnp.float32),
        lax.psum(totals[4].astype(jnp.bfloat16), "rep").astype(jnp.float32),
        lax.psum(totals[5].astype(jnp.bfloat16), "rep").astype(jnp.float32),
        lax.psum(totals[6].astype(jnp.bfloat16), "rep").astype(jnp.float32),
        lax.psum(totals[7].astype(jnp.bfloat16), "rep").astype(jnp.float32),
        lax.psum(totals[8].astype(jnp.bfloat16), "rep").astype(jnp.float32),
        lax.psum(totals[9].astype(jnp.bfloat16), "rep").astype(jnp.float32),
        lax.psum(totals[10].astype(jnp.bfloat16), "rep").astype(jnp.float32),
        lax.psum(totals[11].astype(jnp.bfloat16), "rep").astype(jnp.float32),
        lax.psum(totals[12].astype(jnp.bfloat16), "rep").astype(jnp.float32),
        lax.psum(totals[13].astype(jnp.bfloat16), "rep").astype(jnp.float32),
    )
    table_total = lax.psum(table_total, ("shard", "rep"))
    out_hidden = jnp.stack(results)[:, None]
    grad_hidden = jnp.stack(token_gradient_rows)[:, None]
    grad_encoded = jnp.stack(encoder_grads)[:, None]
    return (
        out_hidden,
        grad_hidden,
        grad_encoded,
        totals[0],
        totals[1],
        totals[2],
        totals[3],
        totals[4],
        table_total,
        totals[5],
        totals[6],
        totals[7],
        totals[8],
        totals[9],
        totals[10],
        totals[11],
        totals[12],
        totals[13],
    )


def solution(mesh):
    return jax.shard_map(
        body,
        mesh=mesh,
        in_specs=(
            P(None, ("shard", "rep"), None, None),
            P(None, ("shard", "rep"), None, None),
            P(None, ("shard", "rep"), None),
            P(None, ("shard", "rep"), None),
            P(),
            P(None, ("shard", "rep"), None, None),
            P("shard"),
            P("shard", None),
            P("shard", None),
            P("shard", None),
            P("shard", None),
            P(),
            P("shard"),
            P("shard", None),
            P("shard", None),
            P("shard", None),
            P("shard", None),
            P("shard"),
            P("shard", None),
            P("shard", None),
            P("shard", None),
        ),
        out_specs=(
            P(None, ("shard", "rep"), None, None),
            P(None, ("shard", "rep"), None, None),
            P(None, ("shard", "rep"), None, None),
            P("shard"),
            P("shard", None),
            P("shard", None),
            P("shard", None),
            P("shard", None),
            P(),
            P("shard"),
            P("shard", None),
            P("shard", None),
            P("shard", None),
            P("shard", None),
            P("shard"),
            P("shard", None),
            P("shard", None),
            P("shard", None),
        ),
        check_vma=False,
    )
```

profile of v0, /device:TPU:0, one launch (start us, length us, event | category | flops | bytes accessed | tf_op | source)
XLA Modules:
  0.0 1705.7 jit_solution(3747264036659084131)
XLA Ops:
  15.6 97.2 %gather_fusion = s32[16384]{0:T(1024)S(1)} fusion(s32[128]{0:T(128)S(1)} %copy-done.2, s32[16384]{0:T(1024)S(1)} %bitcast_clamp_fusion), kind=kCustom, calls=%fused_computation | custom fusion | bytes 196608 | tf_op jit(solution)/shard_map/jit(_take)/gather | solution.py:235
  115.3 36.4 %all-reduce.7 = (bf16[1024]{0:T(1024)(128)(2,1)S(1)}, bf16[1024]{0:T(1024)(128)(2,1)S(1)}, bf16[1024]{0:T(1024)(128)(2,1)S(1)}) all-reduce(bf16[1024]{0:T(1024)(128)(2,1)S(1)} %dynamic-update-slice, bf16[1024]{0:T(1024)(128)(2,1)S(1)} %dynamic-update-slice.1, ...), channel_id=1, replica_groups=mesh['shard'=16,'rep'=2] {'shard'}, use_global_device_ids=true, to_apply=%add | all-reduce | flops 3072 | bytes 12288
  152.5 2.5 convolution_convert_fusion.30
  155.2 2.2 convolution_convert_fusion.29
  157.5 2.2 convolution_convert_fusion.31
  161.9 19.8 %all-gather.18.cloned.1.call-done = bf16[1024,1024]{1,0:T(8,128)(2,1)} async-done(((bf16[64,1024]{1,0:T(8,128)(2,1)}), bf16[1024,1024]{1,0:T(8,128)(2,1)}) %all-gather.18.cloned.1.call-update) | async-done | bytes 2097168 | tf_op jit(solution)/shard_map/all_gather | solution.py:254
  181.7 2.1 multiply_reduce_fusion.15
  183.8 40.0 %all-gather.22.cloned.1.call-done = bf16[1024,1024]{1,0:T(8,128)(2,1)} async-done(((bf16[64,1024]{1,0:T(8,128)(2,1)}), bf16[1024,1024]{1,0:T(8,128)(2,1)}) %all-gather.22.cloned.1.call-update) | async-done | bytes 2097168 | tf_op jit(solution)/shard_map/all_gather | solution.py:256
  223.9 2.1 convolution_convert_fusion.27
  226.2 39.9 %all-gather.24.cloned.1.call-done = bf16[1024,1024]{1,0:T(8,128)(2,1)} async-done(((bf16[64,1024]{1,0:T(8,128)(2,1)}), bf16[1024,1024]{1,0:T(8,128)(2,1)}) %all-gather.24.cloned.1.call-update) | async-done | bytes 2097168 | tf_op jit(solution)/shard_map/all_gather | solution.py:257
  266.1 2.3 convolution_convert_fusion.6
  269.4 39.0 %all-gather.20.cloned.1.call-done = bf16[1024,1024]{1,0:T(8,128)(2,1)} async-done(((bf16[64,1024]{1,0:T(8,128)(2,1)}), bf16[1024,1024]{1,0:T(8,128)(2,1)}) %all-gather.20.cloned.1.call-update) | async-done | bytes 2097168 | tf_op jit(solution)/shard_map/all_gather | solution.py:258
  308.5 3.3 convolution_convert_fusion.7
  316.9 2.8 convolution_convert_fusion.23
  323.9 2.1 fusion.159
  333.0 2.6 convolution_convert_fusion.4
  335.6 2.1 copy.138
  337.6 2.5 convolution_convert_fusion.5
  345.6 5.3 all-gather.26.cloned.1.call-done
  350.8 2.3 multiply_reduce_fusion.14
  358.9 51.6 %all-gather.28.cloned.1.call-done = bf16[1024,2816]{1,0:T(8,128)(2,1)} async-done(((bf16[64,2816]{1,0:T(8,128)(2,1)}), bf16[1024,2816]{1,0:T(8,128)(2,1)}) %all-gather.28.cloned.1.call-update) | async-done | bytes 5767184 | tf_op jit(solution)/shard_map/all_gather | solution.py:261
  410.5 4.7 fusion.161
  415.2 54.8 %all-gather.30.cloned.1.call-done = bf16[1024,2816]{1,0:T(8,128)(2,1)} async-done(((bf16[64,2816]{1,0:T(8,128)(2,1)}), bf16[1024,2816]{1,0:T(8,128)(2,1)}) %all-gather.30.cloned.1.call-update) | async-done | bytes 5767184 | tf_op jit(solution)/shard_map/all_gather | solution.py:262
  470.0 4.7 fusion.162
  474.7 54.9 %all-gather.32.cloned.1.call-done = bf16[2816,1024]{1,0:T(8,128)(2,1)} async-done(((bf16[176,1024]{1,0:T(8,128)(2,1)}), bf16[2816,1024]{1,0:T(8,128)(2,1)}) %all-gather.32.cloned.1.call-update) | async-done | bytes 5767184 | tf_op jit(solution)/shard_map/all_gather | solution.py:263
  529.7 7.1 multiply_convert_fusion.3
  536.8 5.1 fusion.165
  542.0 2.6 multiply_reduce_fusion.5
  548.2 3.7 multiply_convert_fusion.2
  553.9 3.0 multiply_reduce_fusion.4
  562.1 2.1 multiply_reduce_fusion.1
  566.2 2.8 fusion.141
  572.4 2.9 multiply_reduce_fusion
  578.4 2.8 convolution_add_fusion.4
  581.3 2.6 fusion.168
  587.5 2.7 convolution_add_fusion.5
  591.2 3.2 convolution_convert_fusion.17
  596.3 3.4 convolution_convert_fusion.11
  605.8 2.9 convolution_add_fusion.6
  608.7 2.2 multiply_reduce_fusion.3
  614.8 2.8 convolution_add_fusion.7
  619.6 2.7 convolution_add_fusion.3
  626.1 2.8 convolution_add_fusion.8
  633.2 2.7 add_bitcast_fusion
  635.9 5.4 copy.169
  646.1 2.7 add_bitcast_fusion.1
  648.9 5.4 copy.167
  657.1 6.0 convolution_add_fusion.2
  666.0 6.2 convolution_add_fusion.1
  675.2 5.9 convolution_add_fusion
  693.1 3.7 fusion.28
  699.4 29.3 %reduce-scatter.22.cloned.1.call-done = f32[64,1024]{1,0:T(8,128)} async-done(((f32[1024,1024]{1,0:T(8,128)}), f32[64,1024]{1,0:T(8,128)}) %reduce-scatter.22.cloned.1.call-update) | async-done | bytes 262160 | tf_op jit(solution)/shard_map/reduce_scatter | solution.py:288
  730.3 74.0 %reduce-scatter.20.cloned.1.call-done = f32[64,1024]{1,0:T(8,128)} async-done(((f32[1024,1024]{1,0:T(8,128)}), f32[64,1024]{1,0:T(8,128)}) %reduce-scatter.20.cloned.1.call-update) | async-done | bytes 262160 | tf_op jit(solution)/shard_map/reduce_scatter | solution.py:287
  805.9 74.0 %reduce-scatter.18.cloned.1.call-done = f32[64,1024]{1,0:T(8,128)} async-done(((f32[1024,1024]{1,0:T(8,128)}), f32[64,1024]{1,0:T(8,128)}) %reduce-scatter.18.cloned.1.call-update) | async-done | bytes 262160 | tf_op jit(solution)/shard_map/reduce_scatter | solution.py:286
  881.5 74.0 %reduce-scatter.26.cloned.1.call-done = f32[64,1024]{1,0:T(8,128)} async-done(((f32[1024,1024]{1,0:T(8,128)}), f32[64,1024]{1,0:T(8,128)}) %reduce-scatter.26.cloned.1.call-update) | async-done | bytes 262160 | tf_op jit(solution)/shard_map/reduce_scatter | solution.py:293
  957.2 74.0 %reduce-scatter.16.cloned.1.call-done = f32[64,1024]{1,0:T(8,128)} async-done(((f32[1024,1024]{1,0:T(8,128)}), f32[64,1024]{1,0:T(8,128)}) %reduce-scatter.16.cloned.1.call-update) | async-done | bytes 262160 | tf_op jit(solution)/shard_map/reduce_scatter | solution.py:285
  1032.8 73.9 %reduce-scatter.36.cloned.1.call-done = f32[64,1024]{1,0:T(8,128)} async-done(((f32[1024,1024]{1,0:T(8,128)}), f32[64,1024]{1,0:T(8,128)}) %reduce-scatter.36.cloned.1.call-update) | async-done | bytes 262160
  1108.5 73.9 %reduce-scatter.34.cloned.1.call-done = f32[64,1024]{1,0:T(8,128)} async-done(((f32[1024,1024]{1,0:T(8,128)}), f32[64,1024]{1,0:T(8,128)}) %reduce-scatter.34.cloned.1.call-update) | async-done | bytes 262160
  1184.3 128.3 %reduce-scatter.28.cloned.1.call-done = f32[64,2816]{1,0:T(8,128)} async-done(((f32[1024,2816]{1,0:T(8,128)}), f32[64,2816]{1,0:T(8,128)}) %reduce-scatter.28.cloned.1.call-update) | async-done | bytes 720912 | tf_op jit(solution)/shard_map/reduce_scatter | solution.py:295
  1314.4 128.6 %reduce-scatter.30.cloned.1.call-done = f32[64,2816]{1,0:T(8,128)} async-done(((f32[1024,2816]{1,0:T(8,128)}), f32[64,2816]{1,0:T(8,128)}) %reduce-scatter.30.cloned.1.call-update) | async-done | bytes 720912 | tf_op jit(solution)/shard_map/reduce_scatter | solution.py:296
  1444.9 128.5 %reduce-scatter.32.cloned.1.call-done = f32[176,1024]{1,0:T(8,128)} async-done(((f32[2816,1024]{1,0:T(8,128)}), f32[176,1024]{1,0:T(8,128)}) %reduce-scatter.32.cloned.1.call-update) | async-done | bytes 720912 | tf_op jit(solution)/shard_map/reduce_scatter | solution.py:297
  1576.3 59.8 %all-reduce.6 = (bf16[1024]{0:T(1024)(128)(2,1)S(1)}, bf16[1024]{0:T(1024)(128)(2,1)S(1)}, bf16[1024]{0:T(1024)(128)(2,1)S(1)}) all-reduce(f32[1024]{0:T(1024)S(1)} %add.333, f32[1024]{0:T(1024)S(1)} %add.339, f32[1024]{0:T(1024)S(1)} %add.346), channel_id=2, replica_groups=mesh['shard'=16,'rep'=2] {'shard'}, use_global_device_ids=true, to_apply=%region_26.27.clone | all-reduce | flops 3072 | bytes 18432
  1636.3 5.1 all-reduce.8
  1643.0 37.0 %psum.110 = f32[32,16]{0,1:T(8,128)} all-reduce(f32[32,16]{0,1:T(8,128)S(1)} %fusion.31), channel_id=1, replica_groups=mesh['shard'=16,'rep'=2] {'shard','rep'}, use_global_device_ids=true, to_apply=%region_36.37 | all-reduce | flops 512 | bytes 4096 | tf_op jit(solution)/shard_map/psum | solution.py:315
  (533 shorter events, 152.3 us)
Async XLA Ops:
  7.2 144.7 %copy-start = (bf16[32,16]{0,1:T(8,128)(2,1)S(1)}, bf16[32,16]{0,1:T(8,128)(2,1)}, u32[]{:S(2)}) copy-start(bf16[32,16]{0,1:T(8,128)(2,1)} %param.32) | copy-start | bytes 3076
  7.2 7.6 copy-start.7
  7.2 8.3 copy-start.2
  7.2 145.2 %all-gather.14.cloned.1.call-start = ((), (), s32[]{:S(2)}) async-start(), calls=%async_computation.12 | async-start | bytes 2228224 | tf_op jit(solution)/shard_map/all_gather | solution.py:251
  8.0 147.2 %all-gather.16.cloned.1.call-start = ((), (), s32[]{:S(2)}) async-start(), calls=%async_computation.13 | async-start | bytes 2228224 | tf_op jit(solution)/shard_map/all_gather | solution.py:252
  8.7 148.8 %all-gather.12.cloned.1.call-start = ((), (), s32[]{:S(2)}) async-start(), calls=%async_computation.11 | async-start | bytes 2228224 | tf_op jit(solution)/shard_map/all_gather | solution.py:253
  9.4 172.2 %all-gather.18.cloned.1.call-start = ((), (), s32[]{:S(2)}) async-start(), calls=%async_computation.14 | async-start | bytes 2228224 | tf_op jit(solution)/shard_map/all_gather | solution.py:254
  10.0 213.9 %all-gather.22.cloned.1.call-start = ((), (), s32[]{:S(2)}) async-start(), calls=%async_computation.16 | async-start | bytes 2228224 | tf_op jit(solution)/shard_map/all_gather | solution.py:256
  10.6 255.5 %all-gather.24.cloned.1.call-start = ((), (), s32[]{:S(2)}) async-start(), calls=%async_computation.17 | async-start | bytes 2228224 | tf_op jit(solution)/shard_map/all_gather | solution.py:257
  11.2 297.3 %all-gather.20.cloned.1.call-start = ((), (), s32[]{:S(2)}) async-start(), calls=%async_computation.15 | async-start | bytes 2228224 | tf_op jit(solution)/shard_map/all_gather | solution.py:258
  11.9 338.9 %all-gather.26.cloned.1.call-start = ((), (), s32[]{:S(2)}) async-start(), calls=%async_computation.18 | async-start | bytes 2228224 | tf_op jit(solution)/shard_map/all_gather | solution.py:259
  12.7 397.9 %all-gather.28.cloned.1.call-start = ((), (), s32[]{:S(2)}) async-start(), calls=%async_computation.19 | async-start | bytes 6127616 | tf_op jit(solution)/shard_map/all_gather | solution.py:261
  13.4 456.6 %all-gather.30.cloned.1.call-start = ((), (), s32[]{:S(2)}) async-start(), calls=%async_computation.20 | async-start | bytes 6127616 | tf_op jit(solution)/shard_map/all_gather | solution.py:262
  14.0 515.6 %all-gather.32.cloned.1.call-start = ((), (), s32[]{:S(2)}) async-start(), calls=%async_computation.21 | async-start | bytes 6127616 | tf_op jit(solution)/shard_map/all_gather | solution.py:263
  14.7 683.0 %reduce-scatter.24.cloned.1.call-start = ((), (), s32[]{:S(2)}) async-start(), calls=%async_computation.26 | async-start | bytes 4456448 | tf_op jit(solution)/shard_map/reduce_scatter | solution.py:290
  15.0 98.3 %copy-start.144 = (f32[128]{0:T(128)}, f32[128]{0:T(128)S(1)}, u32[]{:S(2)}) copy-start(f32[128]{0:T(128)S(1)} %get-tuple-element.87) | copy-start | bytes 1540
  15.6 97.3 %copy-start.146 = (s32[2,1,128]{2,1,0:T(1,128)S(1)}, s32[2,1,128]{2,1,0:T(1,128)}, u32[]{:S(2)}) copy-start(s32[2,1,128]{2,1,0:T(1,128)} %param.23) | copy-start | bytes 3076
  15.6 97.4 %copy-start.141 = (s32[2,1,256]{2,1,0:T(1,128)S(1)}, s32[2,1,256]{2,1,0:T(1,128)}, u32[]{:S(2)}) copy-start(s32[2,1,256]{2,1,0:T(1,128)} %param.24) | copy-start | bytes 6148
  15.6 97.7 %copy-start.140 = (u32[32]{0:T(128)S(1)}, u32[32]{0:T(128)}, u32[]{:S(2)}) copy-start(u32[32]{0:T(128)} %constant.62) | copy-start | bytes 388
  15.6 99.0 %copy-start.155 = (bf16[64]{0:T(256)(128)(2,1)S(1)}, bf16[64]{0:T(256)(128)(2,1)}, u32[]{:S(2)}) copy-start(bf16[64]{0:T(256)(128)(2,1)} %param.27) | copy-start | bytes 388
  15.6 99.2 %copy-start.156 = (bf16[64]{0:T(256)(128)(2,1)S(1)}, bf16[64]{0:T(256)(128)(2,1)}, u32[]{:S(2)}) copy-start(bf16[64]{0:T(256)(128)(2,1)} %param.33) | copy-start | bytes 388
  15.6 99.5 %copy-start.157 = (bf16[64]{0:T(256)(128)(2,1)S(1)}, bf16[64]{0:T(256)(128)(2,1)}, u32[]{:S(2)}) copy-start(bf16[64]{0:T(256)(128)(2,1)} %param.38) | copy-start | bytes 388
  113.3 208.3 %copy-start.131 = (f32[128]{0:T(128)}, f32[128]{0:T(128)S(1)}, u32[]{:S(2)}) copy-start(f32[128]{0:T(128)S(1)} %fusion.134) | copy-start | bytes 1540
  152.5 7.4 copy-start.40
  161.9 64.1 %copy-start.114 = (bf16[16,64,128]{2,1,0:T(8,128)(2,1)}, bf16[16,64,128]{2,1,0:T(8,128)(2,1)S(1)}, u32[]{:S(2)}) copy-start(bf16[16,64,128]{2,1,0:T(8,128)(2,1)S(1)} %convolution_convert_fusion.28) | copy-start | bytes 786436
  183.8 84.6 %copy-start.151 = (f32[128]{0:T(128)}, f32[128]{0:T(128)S(1)}, u32[]{:S(2)}) copy-start(f32[128]{0:T(128)S(1)} %get-tuple-element.137) | copy-start | bytes 1540
  183.8 82.3 %copy-start.66 = (bf16[2,1,256,1024]{3,2,1,0:T(8,128)(2,1)S(1)}, bf16[2,1,256,1024]{3,2,1,0:T(8,128)(2,1)}, u32[]{:S(2)}) copy-start(bf16[2,1,256,1024]{3,2,1,0:T(8,128)(2,1)} %param.22) | copy-start | bytes 3145732
  226.2 114.9 %copy-start.83 = (bf16[128,1024]{0,1:T(8,128)(2,1)}, bf16[128,1024]{0,1:T(8,128)(2,1)S(1)}, u32[]{:S(2)}) copy-start(bf16[128,1024]{0,1:T(8,128)(2,1)S(1)} %copy.130) | copy-start | bytes 786436
  269.4 44.4 %copy-start.12 = (bf16[1024,1024]{1,0:T(8,128)(2,1)S(1)}, bf16[1024,1024]{1,0:T(8,128)(2,1)}, u32[]{:S(2)}) copy-start(bf16[1024,1024]{1,0:T(8,128)(2,1)} %all-gather.14.cloned.1.call-done) | copy-start | bytes 6291460
  315.0 6.6 copy-start.10
  329.2 6.4 copy-start.153
  345.6 7.6 copy-start.84
  353.1 5.6 copy-start.29
  353.2 5.6 copy-start.138
  536.8 5.2 copy-start.32
  581.2 147.5 %reduce-scatter.22.cloned.1.call-start = ((), (), s32[]{:S(2)}) async-start(), calls=%async_computation.25 | async-start | bytes 4456448 | tf_op jit(solution)/shard_map/reduce_scatter | solution.py:288
  590.2 214.1 %reduce-scatter.20.cloned.1.call-start = ((), (), s32[]{:S(2)}) async-start(), calls=%async_computation.24 | async-start | bytes 4456448 | tf_op jit(solution)/shard_map/reduce_scatter | solution.py:287
  608.7 271.2 %reduce-scatter.18.cloned.1.call-start = ((), (), s32[]{:S(2)}) async-start(), calls=%async_computation.23 | async-start | bytes 4456448 | tf_op jit(solution)/shard_map/reduce_scatter | solution.py:286
  617.7 337.9 %reduce-scatter.26.cloned.1.call-start = ((), (), s32[]{:S(2)}) async-start(), calls=%async_computation.27 | async-start | bytes 4456448 | tf_op jit(solution)/shard_map/reduce_scatter | solution.py:293
  622.3 408.9 %reduce-scatter.16.cloned.1.call-start = ((), (), s32[]{:S(2)}) async-start(), calls=%async_computation.22 | async-start | bytes 4456448 | tf_op jit(solution)/shard_map/reduce_scatter | solution.py:285
  629.0 477.8 %reduce-scatter.36.cloned.1.call-start = ((), (), s32[]{:S(2)}) async-start(), calls=%async_computation.32 | async-start | bytes 4456448
  641.3 541.1 %reduce-scatter.34.cloned.1.call-start = ((), (), s32[]{:S(2)}) async-start(), calls=%async_computation.31 | async-start | bytes 4456448
  654.3 658.2 %reduce-scatter.28.cloned.1.call-start = ((), (), s32[]{:S(2)}) async-start(), calls=%async_computation.28 | async-start | bytes 12255232 | tf_op jit(solution)/shard_map/reduce_scatter | solution.py:295
  663.2 779.8 %reduce-scatter.30.cloned.1.call-start = ((), (), s32[]{:S(2)}) async-start(), calls=%async_computation.29 | async-start | bytes 12255232 | tf_op jit(solution)/shard_map/reduce_scatter | solution.py:296
  672.2 901.3 %reduce-scatter.32.cloned.1.call-start = ((), (), s32[]{:S(2)}) async-start(), calls=%async_computation.30 | async-start | bytes 12255232 | tf_op jit(solution)/shard_map/reduce_scatter | solution.py:297
  681.2 1006.9 %all-reduce.12.cloned.1.call-start = ((), (), s32[]{:S(2)}) async-start(), calls=%async_computation.33 | async-start | bytes 4784128 | tf_op jit(solution)/shard_map/psum | solution.py:307
  690.4 6.4 slice-start.4
  691.3 5.5 slice-start.5
  1444.9 131.3 %copy-start.135 = (f32[1024]{0:T(1024)S(1)}, f32[1024]{0:T(1024)}, u32[]{:S(2)}) copy-start(f32[1024]{0:T(1024)} %get-tuple-element.78) | copy-start | bytes 12292
  1444.9 131.3 %copy-start.136 = (f32[1024]{0:T(1024)S(1)}, f32[1024]{0:T(1024)}, u32[]{:S(2)}) copy-start(f32[1024]{0:T(1024)} %get-tuple-element.121) | copy-start | bytes 12292
  1444.9 131.4 %copy-start.133 = (f32[1024]{0:T(1024)S(1)}, f32[1024]{0:T(1024)}, u32[]{:S(2)}) copy-start(f32[1024]{0:T(1024)} %get-tuple-element.72) | copy-start | bytes 12292
  1444.9 131.4 %copy-start.134 = (f32[1024]{0:T(1024)S(1)}, f32[1024]{0:T(1024)}, u32[]{:S(2)}) copy-start(f32[1024]{0:T(1024)} %get-tuple-element.74) | copy-start | bytes 12292
  1444.9 235.1 %copy-start.143 = (f32[128]{0:T(128)S(1)}, f32[128]{0:T(128)}, u32[]{:S(2)}) copy-start(f32[128]{0:T(128)} %copy-done.142) | copy-start | bytes 1540
  1444.9 235.1 %copy-start.145 = (f32[128]{0:T(128)S(1)}, f32[128]{0:T(128)}, u32[]{:S(2)}) copy-start(f32[128]{0:T(128)} %copy-done.144) | copy-start | bytes 1540
  1444.9 235.1 %copy-start.47 = (f32[128,1024]{1,0:T(8,128)S(1)}, f32[128,1024]{1,0:T(8,128)}, u32[]{:S(2)}) copy-start(f32[128,1024]{1,0:T(8,128)} %copy-done.46) | copy-start | bytes 1572868
  1444.9 235.1 %copy-start.108 = (f32[128,1024]{1,0:T(8,128)S(1)}, f32[128,1024]{1,0:T(8,128)}, u32[]{:S(2)}) copy-start(f32[128,1024]{1,0:T(8,128)} %get-tuple-element.156) | copy-start | bytes 1572868
  1688.1 5.6 copy-start.127
  1688.1 6.3 copy-start.126
  1688.1 7.0 copy-start.125
  1690.1 5.8 copy-start.124
  1690.1 6.5 copy-start.123
  1690.1 7.2 copy-start.122
  1692.0 6.1 copy-start.121
  1692.0 7.0 copy-start.1
  (123 other events, 257.5 us)
Sparse Core Ops, SparseCore 0:
  10.2 44.1 all-gather.13
  56.6 40.1 all-gather.15
  99.0 40.4 all-gather.11
  141.5 40.1 all-gather.17
  183.7 40.1 all-gather.21
  225.9 40.1 all-gather.23
  268.3 40.1 all-gather.19
  310.6 40.1 all-gather.25
  353.1 57.3 all-gather.27
  412.7 57.2 all-gather.29
  472.3 57.2 all-gather.31
  581.3 71.4 reduce-scatter.23
  656.6 71.9 reduce-scatter.21
  732.4 71.8 reduce-scatter.19
  808.0 71.8 reduce-scatter.17
  883.6 71.8 reduce-scatter.25
  959.3 71.8 reduce-scatter.15
  1034.9 71.7 reduce-scatter.35
  1110.6 71.8 reduce-scatter.33
  1186.4 126.0 reduce-scatter.27
  1316.6 126.3 reduce-scatter.29
  1447.1 126.3 reduce-scatter.31
  1578.2 68.9 all-reduce.11
where the time goes:
time: 1710 us
  waiting for transfers between devices  1170 us (68%)
  matrix products  182 us (11%)
  local copies, waits for them, and re-layouts  158 us (9%)
  blocking collectives  138 us (8%)
  other arithmetic  36.7 us (2%)
  between operations  17.9 us (1%)
    unnamed x25, waiting for transfers between devices  155 us
    reduce_scatter x1, waiting for transfers between devices, body(): lax.psum_scatter(totals[12], 'shard', scatter_dimension=0, tiled=True)  129 us
    reduce_scatter x1, waiting for transfers between devices, body(): lax.psum_scatter(totals[13], 'shard', scatter_dimension=0, tiled=True)  129 us
    reduce_scatter x1, waiting for transfers between devices, body(): lax.psum_scatter(totals[11], 'shard', scatter_dimension=0, tiled=True)  128 us
    gather x1, local copies, waits for them, and re-layouts, body(): pair_bucket = jnp.take(buckets, distance)  97.2 us
    unnamed x2, blocking collectives  96.2 us
    reduce_scatter x1, waiting for transfers between devices, body(): lax.psum_scatter(totals[9], 'shard', scatter_dimension=0, tiled=True)  74 us
    reduce_scatter x1, waiting for transfers between devices, body(): lax.psum_scatter(totals[1], 'shard', scatter_dimension=0, tiled=True)  74 us
  transfers between devices with their start and end apart: 23, of which 18 were waited for; matrix products, arithmetic and copies ran while one was open for 17% of the time, Pallas kernels for 0%

commit v1 on v0

v1 whole, which is shorter than its diff:
```python
import functools
import math

import jax
import jax.numpy as jnp
from jax import lax
from jax.experimental import pallas as pl
from jax.experimental.pallas import tpu as pltpu
from jax.sharding import PartitionSpec as P

MESH = pl.DeviceIdType.MESH
BF = jnp.bfloat16
F32 = jnp.float32
EPS = 1e-06
NEG = -1e30
C1 = math.sqrt(2.0 / math.pi)
C2 = 0.044715
TILE = 256


def each(count, f):
    def step(i, carry):
        f(i)
        return carry
    lax.fori_loop(0, count, step, 0)


def tile_at(i, size=TILE):
    return pl.ds(pl.multiple_of(i * size, size), size)


def dot(a, b):
    return jnp.dot(a, b, preferred_element_type=F32)


def dot_t(a, b):
    return lax.dot_general(a, b, (((1,), (1,)), ((), ())), preferred_element_type=F32)


def dot_rows(a, b):
    return lax.dot_general(a, b, (((0,), (0,)), ((), ())), preferred_element_type=F32)


def normed(src, gain, dst):
    def rows(i):
        r = tile_at(i, 32)
        v = src[r, :].astype(F32)
        t = lax.rsqrt(jnp.mean(v * v, axis=-1, keepdims=True) + EPS)
        dst[r, :] = (v * t * gain[...]).astype(BF)
    each(src.shape[0] // 32, rows)


def norm_back(src, gain, grad, base, dst, gain_sum):
    gain_sum[...] = jnp.zeros(gain_sum.shape, F32)

    def rows(i):
        r = tile_at(i, 16)
        v = src[r, :].astype(F32)
        dy = grad[r, :]
        g = gain[...]
        t = lax.rsqrt(jnp.mean(v * v, axis=-1, keepdims=True) + EPS)
        vt = v * t
        gdy = g * dy
        inner = jnp.mean(vt * gdy, axis=-1, keepdims=True)
        dst[r, :] = base[r, :].astype(F32) + t * (gdy - vt * inner)
        gain_sum[...] += jnp.sum(vt * dy, axis=0, keepdims=True)
    each(src.shape[0] // 16, rows)


def turn(src, dst):
    for b in range(src.shape[0] // 128):
        def block(c, b=b):
            dst[tile_at(c), b * 128:(b + 1) * 128] = src[b * 128:(b + 1) * 128, tile_at(c)].T
        each(src.shape[1] // TILE, block)


def head_masks():
    lane = lax.broadcasted_iota(jnp.int32, (1, 128), 1)
    even = (lane < 64).astype(F32).astype(BF)
    return even, (lane >= 64).astype(F32).astype(BF)


def pair_rows(x, masks):
    return jnp.concatenate([x * masks[0], x * masks[1]], axis=0)


def side_by_side(x):
    half = x.shape[0] // 2
    return jnp.concatenate([x[:half], x[half:]], axis=1)


def attend(i, q, k, v, p, o, neg, bias, length, keys):
    masks = head_masks()
    pairs = q.shape[1] // 128
    b, pair = lax.div(i, pairs), lax.rem(i, pairs)
    lanes = tile_at(pair, 128)
    rows, krows = tile_at(b, length), tile_at(b, keys)
    s = dot_t(pair_rows(q[rows, lanes], masks), k[krows, lanes])
    if bias is not None:
        s = s + bias[pair]
    n = neg[b]
    s = s + jnp.concatenate([n, n], axis=0)
    e = jnp.exp(s - jnp.max(s, axis=-1, keepdims=True))
    pb = (e * (1.0 / jnp.sum(e, axis=-1, keepdims=True))).astype(BF)
    p[i] = pb
    o[rows, lanes] = dot(side_by_side(pb), pair_rows(v[krows, lanes], masks)).astype(BF)


def attend_back(i, q, k, v, p, do, dq, dk, dv, diag, length, keys):
    masks = head_masks()
    pairs = q.shape[1] // 128
    b, pair = lax.div(i, pairs), lax.rem(i, pairs)
    lanes = tile_at(pair, 128)
    rows, krows = tile_at(b, length), tile_at(b, keys)
    dos = pair_rows(do[rows, lanes], masks)
    dp = dot_t(dos, v[krows, lanes])
    pb = p[i]
    pf = pb.astype(F32)
    ds = (pf * (dp - jnp.sum(pf * dp, axis=-1, keepdims=True))).astype(BF)
    dq[rows, lanes] = dot(side_by_side(ds), pair_rows(k[krows, lanes], masks)).astype(BF)
    dk[krows, lanes] = dot_rows(ds, pair_rows(q[rows, lanes], masks)).astype(BF)
    dv[krows, lanes] = dot_rows(pb, dos).astype(BF)
    if diag is not None:
        i0 = lax.broadcasted_iota(jnp.int32, (length, length), 0)
        i1 = lax.broadcasted_iota(jnp.int32, (length, length), 1)
        flip = (i0 + i1 == length - 1).astype(F32).astype(BF)
        for h in range(2):
            u = pltpu.roll(dot(flip, ds[h * length:(h + 1) * length]), 1, 1, stride=1, stride_axis=0)
            diag[2 * pair + h] += jnp.sum(u, axis=0, keepdims=True)


def position_bias(taps, bias, length):
    def pair(i):
        for h in range(2):
            w = jnp.broadcast_to(taps[2 * i + h], (length, length))
            bias[i, h * length:(h + 1) * length, :] = pltpu.roll(w, 0, 1, stride=1, stride_axis=0)
    each(bias.shape[0], pair)


def seg_masks(dcol, drow, erow, neg_self, neg_cross, length):
    for b in range(dcol.shape[0]):
        col = dcol[b]
        i = lax.broadcasted_iota(jnp.int32, (length, length), 0)
        j = lax.broadcasted_iota(jnp.int32, (length, length), 1)
        neg_self[b] = jnp.where((j <= i) & (col == drow[b]), 0.0, NEG)
        neg_cross[b] = jnp.where(col == erow[b], 0.0, NEG)


def project(a, w, dst, base=None, kind=BF):
    def tile(c):
        v = dot(a[...], w[:, tile_at(c)])
        if base is not None:
            v = v + base[:, tile_at(c)].astype(F32)
        dst[:, tile_at(c)] = v.astype(kind)
    each(dst.shape[1] // TILE, tile)


def project_t(terms, dst, kind=F32):
    def tile(c):
        v = None
        for a, w in terms:
            u = dot_t(a[...], w[tile_at(c), :])
            v = u if v is None else v + u
        dst[:, tile_at(c)] = v.astype(kind)
    each(dst.shape[1] // TILE, tile)


def feed_tile(c, h, cot, wg, wu, wd, hid, dgate, dup):
    cols = tile_at(c)
    hv = h[...]
    gate = dot(hv, wg[:, cols])
    up = dot(hv, wu[:, cols])
    dhid = dot_t(cot[...], wd[cols, :])
    sq = gate * gate
    th = jnp.tanh(C1 * gate * (1.0 + C2 * sq))
    hp = 0.5 * (1.0 + th)
    act = gate * hp
    hid[:, cols] = (act * up).astype(BF)
    slope = hp + (0.5 * C1) * gate * (1.0 - th * th) * (1.0 + (3.0 * C2) * sq)
    dgate[:, cols] = (dhid * up * slope).astype(BF)
    dup[:, cols] = (dhid * act).astype(BF)


def geometry(n):
    chips = n // 2
    side = chips // 2
    s = lax.axis_index("shard")
    rep = lax.axis_index("rep")
    core = lax.rem(s, 2)
    chip = lax.div(s, 2)
    x = lax.rem(chip, 2)
    z = lax.div(chip, 2)
    ring = z + x * (chips - 1 - 2 * z)

    def device_at(position):
        p = lax.rem(position + 2 * chips, chips)
        px = lax.div(p, side)
        pz = p + px * (chips - 1 - 2 * p)
        return (pz * 2 + px) * 2 + core

    return chips, s, rep, core, ring, device_at


def rdma(src, dst, ss, rs, dev):
    return pltpu.make_async_remote_copy(src_ref=src, dst_ref=dst, send_sem=ss, recv_sem=rs, device_id=dev, device_id_type=MESH)


class Gather:
    def __init__(self, geo, pieces, across, sems):
        self.chips, self.me, self.rep, self.core, self.ring, self.device_at = geo
        self.hops = self.chips - 1
        self.pieces, self.across = pieces, across
        self.ring_s, self.ring_r, self.sib_s, self.sib_r, self.y_s, self.y_r, self.yy_s, self.yy_r, self.own_s, self.own_r = sems
        self.other = 1 - 2 * self.core
        self.sibling = (self.me + self.other, self.rep)
        self.opposite = (self.me, 1 - self.rep)
        self.ahead = ((self.device_at(self.ring + 1), self.rep), (self.device_at(self.ring - 1), self.rep))

    def source(self, way, t):
        return self.device_at(self.ring - 1 - t) if way == 0 else self.device_at(self.ring + 1 + t)

    def each(self, rep, count=None):
        most = max(len(self.pieces(0, rep)), len(self.pieces(1, rep)))
        for p in range(most if count is None else count):
            for way in range(2):
                ps = self.pieces(way, rep)
                if p < len(ps):
                    yield way, p, ps[p]

    def ring_copy(self, way, t, p, ref):
        return rdma(ref, ref, self.ring_s.at[way, t, p], self.ring_r.at[way, t, p], self.ahead[way])

    def sib_copy(self, way, t, p, ref):
        return rdma(ref, ref, self.sib_s.at[way, t, p], self.sib_r.at[way, t, p], self.sibling)

    def y_copy(self, way, t, p, ref):
        return rdma(ref, ref, self.y_s.at[way, t, p], self.y_r.at[way, t, p], self.opposite)

    def yy_copy(self, way, t, p, ref):
        return rdma(ref, ref, self.yy_s.at[way, t, p], self.yy_r.at[way, t, p], self.sibling)

    def own_copies(self, src):
        found = []
        for rep in (self.rep, 1 - self.rep):
            for way, p, ref in self.each(rep, None if rep is self.rep else self.across):
                i = 0 if rep is self.rep else 1
                r = ref(src)
                found.append(rdma(r, r, self.own_s.at[i, way, p], self.own_r.at[i, way, p], self.sibling))
        return found

    def start(self):
        for way, p, ref in self.each(self.rep):
            self.ring_copy(way, 0, p, ref(self.me)).start()
        for c in self.own_copies(self.me):
            c.start()

    def hop(self, t, last=False):
        for way, p, ref in self.each(self.rep):
            r = ref(self.source(way, t))
            self.ring_copy(way, t, p, r).wait_recv()
            if not last:
                self.ring_copy(way, t + 1, p, r).start()
            if p < self.across:
                self.y_copy(way, t, p, r).start()
            self.sib_copy(way, t, p, r).start()

    def relay(self, t):
        for way, p, ref in self.each(1 - self.rep, self.across):
            r = ref(self.source(way, t))
            self.y_copy(way, t, p, r).wait_recv()
            self.yy_copy(way, t, p, r).start()

    def complete(self):
        def step(t):
            for way, p, ref in self.each(self.rep):
                self.sib_copy(way, t, p, ref(self.source(way, t) + self.other)).wait_recv()
            for way, p, ref in self.each(1 - self.rep, self.across):
                self.yy_copy(way, t, p, ref(self.source(way, t) + self.other)).wait_recv()
        each(self.hops, step)
        for c in self.own_copies(self.me + self.other):
            c.wait_recv()

    def drain(self):
        def step(t):
            for way, p, ref in self.each(self.rep):
                r = ref(self.source(way, t))
                self.ring_copy(way, t, p, r).wait_send()
                self.sib_copy(way, t, p, r).wait_send()
                if p < self.across:
                    self.y_copy(way, t, p, r).wait_send()
            for way, p, ref in self.each(1 - self.rep, self.across):
                self.yy_copy(way, t, p, ref(self.source(way, t))).wait_send()
        each(self.hops, step)
        for c in self.own_copies(self.me):
            c.wait_send()


def gather_sems(hops, pieces, across):
    dma = pltpu.SemaphoreType.DMA
    return [dma((2, hops, pieces))] * 4 + [dma((2, hops, across))] * 4 + [dma((2, 2, pieces))] * 2


def forward_kernel(n, dims, *refs):
    length, keys = dims
    ins, refs = refs[:11], refs[11:]
    gn_in, x, enc, cot, dcol, drow, erow, taps = refs[:8]
    w_out, out, xt, enct, hfft, hidt, dgu, r1, x1, qkv, cq, ckv, p1, p2, gain3, gains = refs[8:24]
    w, gu, dn, gn, bias, neg_s, neg_c, h, hid, x2, dh, o = refs[24:36]
    first_sems, second_sems = refs[36:46], refs[46:56]
    load_s, store_s = refs[56:58]
    geo = geometry(n)
    chips, me, rep, core, ring, device_at = geo
    hops = chips - 1
    rows, rows_d = ins[0].shape[0], ins[10].shape[0]
    half, half_g = w.shape[2] // 2, gu.shape[2] // 2
    count = dcol.shape[0]
    pairs = w.shape[2] // 128

    def block(src):
        return pl.ds(pl.multiple_of(src * rows, rows), rows)

    def block_d(src):
        return pl.ds(pl.multiple_of(src * rows_d, rows_d), rows_d)

    def attention_pieces(way, r):
        c = pl.ds(way * half, half)
        found = [lambda s: w.at[r, block(s), c], lambda s: w.at[4 + r, block(s), c],
                 lambda s: w.at[pl.ds(2, 2), block(s), c], lambda s: w.at[pl.ds(6, 2), block(s), c]]
        return found + [lambda s: gn.at[s]] if way == 0 else found

    def feed_pieces(way, r):
        return [lambda s: gu.at[r, block(s), pl.ds(way * half_g, half_g)], lambda s: dn.at[block_d(s), pl.ds(way * half, half)]]

    first = Gather(geo, attention_pieces, 2, first_sems)
    second = Gather(geo, feed_pieces, 1, second_sems)

    places = [w.at[i, block(me), :] for i in range(8)] + [gu.at[i, block(me), :] for i in range(2)] + [dn.at[block_d(me), :]]
    loads = [pltpu.make_async_copy(a, b, load_s.at[i]) for i, (a, b) in enumerate(zip(ins + (gn_in,), places + [gn.at[me]]))]
    for c in loads:
        c.start()
    barrier = pltpu.get_barrier_semaphore()
    for dev in first.ahead + (first.sibling, first.opposite):
        pl.semaphore_signal(barrier, inc=1, device_id=dev, device_id_type=MESH)
    for c in loads:
        c.wait()
    pl.semaphore_wait(barrier, 4)

    first.start()
    turn(enc, enct)
    first.hop(0)
    position_bias(taps, bias, length)
    seg_masks(dcol, drow, erow, neg_s, neg_c, length)

    def middle(t):
        first.hop(t)
        first.relay(t - 1)
    lax.fori_loop(1, hops - 1, lambda t, c: (middle(t), c)[1], 0)
    second.start()
    first.hop(hops - 1, True)
    first.relay(hops - 2)
    first.relay(hops - 1)
    first.complete()
    store = pltpu.make_async_copy(w, w_out, store_s)
    store.start()

    per = 128 // rows
    for j in range(w.shape[2] // 128):
        v = gn[j * per]
        for i in range(1, per):
            v = v + gn[j * per + i]
        for i in range(3):
            gains[i, :, j * 128:(j + 1) * 128] = v[i:i + 1, :]

    def some(begin, end, f):
        lax.fori_loop(begin, end, lambda i, c: (f(i), c)[1], 0)

    def heads():
        normed(x, gains.at[0], h)
        for i in range(3):
            project(h, w.at[i], qkv.at[i])

    def own(i):
        attend(i, qkv.at[0], qkv.at[1], qkv.at[2], p1, o, neg_s, bias, length, length)

    def cross_heads():
        turn(h, xt.at[0])
        turn(o, xt.at[1])
        project(o, w.at[3], x1, base=x, kind=F32)
        normed(x1, gains.at[1], h)
        project(h, w.at[4], cq)

    def cross_keys():
        turn(h, xt.at[2])
        for i in range(2):
            project(enc, w.at[6 + i], ckv.at[i])

    def cross(i):
        attend(i, cq, ckv.at[0], ckv.at[1], p2, o, neg_c, None, length, keys)

    def before_feed():
        turn(o, xt.at[3])
        project(o, w.at[5], x2, base=x1, kind=F32)
        normed(x2, gains.at[2], h)
        turn(h, hfft)

    total = count * pairs
    mid = total // 2
    chunks = [heads, lambda: some(0, mid, own), lambda: some(mid, total, own), cross_heads, cross_keys,
              lambda: some(0, mid, cross), lambda: some(mid, total, cross)]
    for t in range(len(chunks)):
        chunks[t]()
        second.hop(t, t == hops - 1)
        if t > 0:
            second.relay(t - 1)
    if hops > len(chunks):
        def rest(t):
            second.hop(t)
            second.relay(t - 1)
        some(len(chunks), hops - 1, rest)
        second.hop(hops - 1, True)
        second.relay(hops - 2)
    before_feed()
    second.relay(hops - 1)
    second.complete()

    each(hid.shape[1] // TILE, lambda c: feed_tile(c, h, cot, gu.at[0], gu.at[1], dn, hid, dgu.at[0], dgu.at[1]))
    project_t([(dgu.at[0], gu.at[0]), (dgu.at[1], gu.at[1])], dh)
    norm_back(x2, gains.at[2], dh, cot, r1, gain3)
    project(hid, dn, out, base=x2)
    turn(hid, hidt)
    first.drain()
    second.drain()
    store.wait()


def forward(n, weights, gn, x, enc, cot, dcol, drow, erow, taps):
    hops = n // 2 - 1
    rows, width = weights[0].shape
    ff = weights[8].shape[1]
    tokens, etokens = x.shape[0], enc.shape[0]
    count, length, _ = dcol.shape
    keys = etokens // count
    pairs = width // 128
    S = jax.ShapeDtypeStruct

    def v(*shape, t=BF):
        return pltpu.VMEM(shape, t)

    vm, hbm = pl.BlockSpec(memory_space=pltpu.VMEM), pl.BlockSpec(memory_space=pl.ANY)
    return pl.pallas_call(
        functools.partial(forward_kernel, n, (length, keys)),
        name="gather_forward",
        out_shape=(
            S((8, width, width), BF), S((tokens, width), BF), S((4, width, tokens), BF), S((width, etokens), BF),
            S((width, tokens), BF), S((ff, tokens), BF), S((2, tokens, ff), BF), S((tokens, width), F32), S((tokens, width), F32),
            S((3, tokens, width), BF), S((tokens, width), BF), S((2, etokens, width), BF),
            S((count * pairs, 2 * length, length), BF), S((count * pairs, 2 * length, keys), BF),
            S((1, width), F32), S((3, 1, width), F32),
        ),
        in_specs=[hbm] * 12 + [vm] * 7,
        out_specs=[hbm] + [vm] * 15,
        scratch_shapes=[
            v(8, width, width), v(2, width, ff), v(ff, width), v(n, 8, 128, t=F32),
            v(pairs, 2 * length, length, t=F32), v(count, length, length, t=F32), v(count, length, keys, t=F32),
            v(tokens, width), v(tokens, ff), v(tokens, width, t=F32), v(tokens, width, t=F32), v(tokens, width),
        ] + gather_sems(hops, 5, 2) + gather_sems(hops, 2, 1) + [pltpu.SemaphoreType.DMA((12,)), pltpu.SemaphoreType.DMA(())],
        compiler_params=pltpu.CompilerParams(collective_id=0, has_side_effects=True, vmem_limit_bytes=67043328),
    )(*weights, gn, x, enc, cot, dcol, drow, erow, taps)


def backward_kernel(dims, *refs):
    length, keys = dims
    x, w, gains, r1, x1, qkv, cq, ckv, p1, p2, dtok, denc, dy, dye, gain12, diag, dh, r0, do = refs
    diag[...] = jnp.zeros(diag.shape, F32)
    total = p1.shape[0]
    dy[5] = r1[...].astype(BF)
    project_t([(dy.at[5], w.at[5])], do, kind=BF)
    each(total, lambda i: attend_back(i, cq, ckv.at[0], ckv.at[1], p2, do, dy.at[4], dye.at[0], dye.at[1], None, length, keys))
    project_t([(dye.at[0], w.at[6]), (dye.at[1], w.at[7])], denc)
    project_t([(dy.at[4], w.at[4])], dh)
    norm_back(x1, gains.at[1], dh, r1, r0, gain12.at[1])
    dy[3] = r0[...].astype(BF)
    project_t([(dy.at[3], w.at[3])], do, kind=BF)
    each(total, lambda i: attend_back(i, qkv.at[0], qkv.at[1], qkv.at[2], p1, do, dy.at[0], dy.at[1], dy.at[2], diag, length, length))
    project_t([(dy.at[0], w.at[0]), (dy.at[1], w.at[1]), (dy.at[2], w.at[2])], dh)
    norm_back(x, gains.at[0], dh, r0, dtok, gain12.at[0])


def backward(x, w, gains, r1, x1, qkv, cq, ckv, p1, p2):
    tokens, width = x.shape
    etokens = ckv.shape[1]
    length, keys = p1.shape[2], p2.shape[2]
    S = jax.ShapeDtypeStruct
    vm = pl.BlockSpec(memory_space=pltpu.VMEM)
    return pl.pallas_call(
        functools.partial(backward_kernel, (length, keys)),
        name="attention_backward",
        out_shape=(S((tokens, width), F32), S((etokens, width), F32), S((6, tokens, width), BF), S((2, etokens, width), BF),
                   S((2, 1, width), F32), S((width // 64, 1, 128), F32)),
        in_specs=[vm] * 10,
        out_specs=[vm] * 6,
        scratch_shapes=[pltpu.VMEM((tokens, width), F32), pltpu.VMEM((tokens, width), F32), pltpu.VMEM((tokens, width), BF)],
        compiler_params=pltpu.CompilerParams(vmem_limit_bytes=67043328),
    )(x, w, gains, r1, x1, qkv, cq, ckv, p1, p2)


class Group:
    def __init__(self, left, right, size, refs):
        self.left, self.right = left, right
        self.count, self.rows, self.half, self.share = size
        self.ss, self.sr, self.ys, self.yr, self.rs, self.rr, self.own, self.got = refs

    def part(self, i, dev, start, width):
        return dot(self.left(i, dev), self.right(i, pl.ds(pl.multiple_of(start, 128), width)))


def group_shapes(size, slots):
    count, rows, half, share = size
    sib_slots, y_slots, ring_slots = slots

    def v(*shape):
        return pltpu.VMEM(shape, BF)
    return [v(2, 2, count, rows, half), v(sib_slots, 2, count, rows, half), v(2, 2, count, rows, share), v(y_slots, 2, count, rows, share),
            v(2, 2, count, rows, half - share), v(ring_slots, 2, count, rows, half - share)]


def reduce_sems(groups, slots):
    dma = pltpu.SemaphoreType.DMA
    sib_slots, y_slots, ring_slots = slots
    return [dma((2, 2, groups)), dma((sib_slots, 2, groups)), dma((2, 2, groups)), dma((y_slots, 2, groups)),
            dma((2, 2, groups)), dma((ring_slots, 2, groups)), dma((2, 2 * groups)), dma((2, 2 * groups)),
            pltpu.SemaphoreType.REGULAR((3, 2))]


class Reduce:
    def __init__(self, geo, groups, slots, sems):
        self.chips, self.me, self.rep, self.core, self.ring, self.device_at = geo
        self.groups = groups
        self.slots = slots
        self.sib_s, self.sib_r, self.y_s, self.y_r, self.ring_s, self.ring_r, self.fin_s, self.fin_r, self.free = sems
        self.other = 1 - self.rep
        self.sibling = (self.me + 1 - 2 * self.core, self.rep)
        self.opposite = (self.me, self.other)
        self.after = ((self.device_at(self.ring + 1), self.rep), (self.device_at(self.ring - 1), self.rep))

    def block(self, t, way, core):
        return self.device_at(self.ring + (2 * way - 1) * (1 + t)) + core - self.core

    def toward(self, way):
        return (self.after[0][0] + way * (self.after[1][0] - self.after[0][0]), self.rep)

    def behind(self, way):
        return (self.after[1][0] + way * (self.after[0][0] - self.after[1][0]), self.rep)

    def sib_copies(self, t, way):
        s, r = lax.rem(t, 2), lax.rem(t, self.slots[0])
        return [rdma(g.ss.at[s, way], g.sr.at[r, way], self.sib_s.at[s, way, i], self.sib_r.at[r, way, i], self.sibling)
                for i, g in enumerate(self.groups)]

    def y_copies(self, t, way):
        s, r = lax.rem(t, 2), lax.rem(t, self.slots[1])
        return [rdma(g.ys.at[s, way], g.yr.at[r, way], self.y_s.at[s, way, i], self.y_r.at[r, way, i], self.opposite)
                for i, g in enumerate(self.groups)]

    def ring_copies(self, t, way):
        s, r = lax.rem(t, 2), lax.rem(t + 1, self.slots[2])
        return [rdma(g.rs.at[s, way], g.rr.at[r, way], self.ring_s.at[s, way, i], self.ring_r.at[r, way, i], self.toward(way))
                for i, g in enumerate(self.groups)]

    def claim(self, kind, step, way):
        if self.slots[kind] < self.chips:
            @pl.when(step >= self.slots[kind])
            def _():
                pl.semaphore_wait(self.free.at[kind, way], 1)

    def release(self, kind, step, way, dev):
        if self.slots[kind] < self.chips:
            @pl.when(step + self.slots[kind] < self.chips)
            def _():
                pl.semaphore_signal(self.free.at[kind, way], inc=1, device_id=dev, device_id_type=MESH)

    def settle(self, t, copies):
        @pl.when(t >= 2)
        def _():
            for c in copies:
                c.wait_send()

    def to_sibling(self, t):
        s = lax.rem(t, 2)

        def go(way):
            dev = self.block(t, way, 1 - self.core)
            self.settle(t, self.sib_copies(t, way))
            for g in self.groups:
                for i in range(g.count):
                    g.ss[s, way, i] = g.part(i, dev, way * g.half, g.half).astype(BF)
            self.claim(0, t, way)
            for c in self.sib_copies(t, way):
                c.start()
        each(2, go)

    def to_across(self, t):
        s, r = lax.rem(t, 2), lax.rem(t, self.slots[0])

        def go(way):
            dev = self.block(t, way, self.core)
            self.settle(t, self.y_copies(t, way))
            for c in self.sib_copies(t, way):
                c.wait_recv()
            for g in self.groups:
                at = pl.multiple_of(self.other * g.share, 128)
                for i in range(g.count):
                    v = g.part(i, dev, way * g.half + at, g.share)
                    g.ys[s, way, i] = (v + g.sr[r, way, i, :, pl.ds(at, g.share)].astype(F32)).astype(BF)
            self.claim(1, t, way)
            for c in self.y_copies(t, way):
                c.start()
        each(2, go)

    def to_ring(self, t):
        s, b, y, r = lax.rem(t, 2), lax.rem(t, self.slots[0]), lax.rem(t, self.slots[1]), lax.rem(t, self.slots[2])

        for k, g in enumerate(self.groups):
            def go(way, k=k, g=g):
                dev = self.block(t, way, self.core)
                self.settle(t, self.ring_copies(t, way)[k:k + 1])
                self.y_copies(t, way)[k].wait_recv()

                @pl.when(t >= 1)
                def _():
                    self.ring_copies(t - 1, way)[k].wait_recv()
                at = pl.multiple_of(self.rep * g.share, 128)
                for i in range(g.count):
                    v = g.part(i, dev, way * g.half + at, g.share) + g.sr[b, way, i, :, pl.ds(at, g.share)].astype(F32)
                    v = v + g.yr[y, way, i].astype(F32) + g.rr[r, way, i, :, :g.share].astype(F32)
                    g.rs[s, way, i, :, :g.share] = v.astype(BF)
                    v = g.part(i, dev, way * g.half + 2 * g.share, g.half - 2 * g.share)
                    v = v + g.sr[b, way, i, :, 2 * g.share:].astype(F32) + g.rr[r, way, i, :, g.share:].astype(F32)
                    g.rs[s, way, i, :, g.share:] = v.astype(BF)

                @pl.when(t < self.chips - 1)
                def _():
                    if k == 0:
                        self.claim(2, t + 1, way)
                    self.ring_copies(t, way)[k].start()
                if k == len(self.groups) - 1:
                    self.release(0, t, way, self.sibling)
                    self.release(1, t, way, self.opposite)
                    self.release(2, t, way, self.behind(way))
            each(2, go)

    def prepare(self):
        for g in self.groups:
            g.rr[0] = jnp.zeros(g.rr.shape[1:], BF)

    def final_copies(self):
        s = (self.chips - 1) % 2
        found = []
        for way in range(2):
            for i, g in enumerate(self.groups):
                mine = g.rs.at[s, way]
                cols = pl.ds(pl.multiple_of(way * g.half + self.rep * g.share, 128), g.share)
                wide = g.half - 2 * g.share
                found.append(rdma(mine.at[:, :, pl.ds(0, g.share)], g.own.at[:, :, cols],
                                  self.fin_s.at[way, 2 * i], self.fin_r.at[way, 2 * i], self.opposite))
                found.append(rdma(mine.at[:, :, pl.ds(g.share, wide)], g.got.at[:, :, pl.ds(way * wide, wide)],
                                  self.fin_s.at[way, 2 * i + 1], self.fin_r.at[way, 2 * i + 1], self.opposite))
        return found

    def send_finals(self):
        s = (self.chips - 1) % 2
        for c in self.final_copies():
            c.start()
        for way in range(2):
            for g in self.groups:
                cols = pl.ds(pl.multiple_of(way * g.half + self.rep * g.share, 128), g.share)
                g.own[:, :, cols] = g.rs[s, way, :, :, :g.share]
                g.own[:, :, way * g.half + 2 * g.share:(way + 1) * g.half] = g.rs[s, way, :, :, g.share:]

    def finish(self):
        for way in range(2):
            for i, g in enumerate(self.groups):
                wide = g.half - 2 * g.share
                ref = g.own.at[:, :, pl.ds(pl.multiple_of(way * g.half + self.other * g.share, 128), g.share)]
                rdma(ref, ref, self.fin_s.at[way, 2 * i], self.fin_r.at[way, 2 * i], self.opposite).wait_recv()
                ref = g.got.at[:, :, pl.ds(way * wide, wide)]
                rdma(ref, ref, self.fin_s.at[way, 2 * i + 1], self.fin_r.at[way, 2 * i + 1], self.opposite).wait_recv()
        for c in self.final_copies():
            c.wait_send()
        for way in range(2):
            for t in (self.chips - 2, self.chips - 1):
                for c in self.sib_copies(t, way) + self.y_copies(t, way):
                    c.wait_send()
            for c in self.ring_copies(self.chips - 2, way):
                c.wait_send()


class Butterfly:
    def __init__(self, geo, n, buf, got, sems):
        _, self.me, self.rep, _, _, _ = geo
        self.stages = n.bit_length() - 1
        self.buf, self.got = buf, got
        self.send, self.recv = sems

    def partner(self, bit):
        return (self.me + bit - 2 * bit * lax.rem(lax.div(self.me, bit), 2), self.rep)

    def copy(self, j, dev):
        return rdma(self.buf.at[j], self.got.at[j], self.send.at[j], self.recv.at[j], dev)

    def begin(self):
        self.copy(0, (self.me, 1 - self.rep)).start()

    def stage(self, j, bit):
        self.copy(j - 1, self.partner(bit)).wait_recv()
        self.buf[j] = self.buf[j - 1] + self.got[j - 1]
        self.copy(j, self.partner(bit)).start()

    def end(self, dst):
        self.copy(self.stages, self.partner(1)).wait_recv()
        dst[...] = self.buf[self.stages] + self.got[self.stages]
        for j in range(self.stages + 1):
            self.copy(j, self.partner(1)).wait_send()


def reduce_kernel(n, sizes, slots, *refs):
    xt, enct, hfft, hidt, dy, dye, dgu, cot, small = refs[:9]
    outs, small_o = refs[9:17], refs[17]
    bufs, sems = refs[18:42], refs[42:51]
    sm, sm_got, sm_s, sm_r = refs[51:]
    geo = geometry(n)
    chips, me, rep, core, ring, device_at = geo
    rows, rows_d = sizes[0][1], sizes[3][1]
    which = (0, 0, 0, 1, 2, 3)

    def block(dev, size):
        return pl.ds(pl.multiple_of(dev * size, size), size)
    lefts = [lambda i, dev: xt[which[i], block(dev, rows), :], lambda i, dev: enct[block(dev, rows), :],
             lambda i, dev: hfft[block(dev, rows), :], lambda i, dev: hidt[block(dev, rows_d), :]]
    rights = [lambda i, c: dy[i, :, c], lambda i, c: dye[i, :, c], lambda i, c: dgu[i, :, c], lambda i, c: cot[:, c]]
    groups = [Group(lefts[k], rights[k], sizes[k], bufs[6 * k:6 * k + 6] + outs[2 * k:2 * k + 2]) for k in range(4)]
    red = Reduce(geo, groups, slots, sems)
    tree = Butterfly(geo, n, sm, sm_got, (sm_s, sm_r))

    barrier = pltpu.get_barrier_semaphore()
    greet = [red.after[0], red.after[1], red.sibling, red.opposite] + [tree.partner(1 << j) for j in range(tree.stages)]
    for dev in greet:
        pl.semaphore_signal(barrier, inc=1, device_id=dev, device_id_type=MESH)
    pl.semaphore_wait(barrier, len(greet))

    red.prepare()
    sm[0] = small[...]
    tree.begin()
    red.to_sibling(0)
    red.to_sibling(1)
    red.to_across(0)
    red.to_sibling(2)
    red.to_across(1)

    def step(t, bit):
        red.to_ring(t)

        @pl.when(t + 2 < chips)
        def _():
            red.to_across(t + 2)

        @pl.when(t + 3 < chips)
        def _():
            red.to_sibling(t + 3)

        @pl.when(t < tree.stages)
        def _():
            tree.stage(t + 1, bit)
        return bit * 2

    lax.fori_loop(0, chips, step, 1)
    red.send_finals()
    tree.end(small_o)
    red.finish()


def shares(half):
    return max(1, half // 512) * 128


def reduce_grads(n, xt, enct, hfft, hidt, dy, dye, dgu, cot, small):
    chips = n // 2
    width, ff = dy.shape[2], dgu.shape[2]
    rows, rows_d = width // n, hidt.shape[0] // n
    sizes = [(6, rows, width // 2, shares(width // 2)), (2, rows, width // 2, shares(width // 2)),
             (2, rows, ff // 2, shares(ff // 2)), (1, rows_d, width // 2, shares(width // 2))]
    slots = (chips, chips, chips)
    stages = n.bit_length() - 1
    dma = pltpu.SemaphoreType.DMA
    S = jax.ShapeDtypeStruct
    vm = pl.BlockSpec(memory_space=pltpu.VMEM)
    outs = []
    for count, r, half, share in sizes:
        outs += [S((count, r, 2 * half), BF), S((count, r, 2 * (half - 2 * share)), BF)]
    return pl.pallas_call(
        functools.partial(reduce_kernel, n, sizes, slots),
        name="reduce_grads",
        out_shape=tuple(outs) + (S(small.shape, F32),),
        in_specs=[vm] * 9,
        out_specs=[vm] * 9,
        scratch_shapes=[b for size in sizes for b in group_shapes(size, slots)] + reduce_sems(4, slots)
        + [pltpu.VMEM((stages + 1,) + small.shape, F32)] * 2 + [dma((stages + 1,))] * 2,
        compiler_params=pltpu.CompilerParams(collective_id=1, has_side_effects=True, vmem_limit_bytes=67043328),
    )(xt, enct, hfft, hidt, dy, dye, dgu, cot, small)


def finish_kernel(sizes, *refs):
    at = 8
    for k, (count, rows, half, share) in enumerate(sizes):
        own, got = refs[2 * k], refs[2 * k + 1]
        wide = half - 2 * share
        for i in range(count):
            dst = refs[at]
            at += 1
            for way in range(2):
                lo = way * half
                dst[:, lo:lo + 2 * share] = own[i, :, lo:lo + 2 * share].astype(F32)
                v = own[i, :, lo + 2 * share:lo + half].astype(F32) + got[i, :, way * wide:(way + 1) * wide].astype(F32)
                dst[:, lo + 2 * share:lo + half] = v


def finish_grads(parts):
    sizes, outs = [], []
    for own, got in zip(parts[0::2], parts[1::2]):
        count, rows, width = own.shape
        half = width // 2
        sizes.append((count, rows, half, (half - got.shape[2] // 2) // 2))
        outs += [jax.ShapeDtypeStruct((rows, width), F32)] * count
    vm = pl.BlockSpec(memory_space=pltpu.VMEM)
    return pl.pallas_call(
        functools.partial(finish_kernel, sizes),
        name="finish_grads",
        out_shape=tuple(outs),
        in_specs=[vm] * len(parts),
        out_specs=[vm] * len(outs),
        compiler_params=pltpu.CompilerParams(vmem_limit_bytes=40 << 20),
    )(*parts)


def body(hidden_in, encoded, dec_segments, enc_segments, buckets, out_cot, norm_self, self_query, self_key, self_value,
         self_out, table, norm_cross, cross_query, cross_key, cross_value, cross_out, norm_ff, ff_gate, ff_up, ff_down, *, n):
    micro, per, length, width = hidden_in.shape
    keys = encoded.shape[2]
    count = micro * per
    rows, rows_d, ff = self_query.shape[0], ff_down.shape[0], ff_gate.shape[1]
    me = lax.axis_index("shard")
    spare = -rows_d % 16
    if spare:
        ff_down = jnp.pad(ff_down, ((0, spare), (0, 0)))
        ff_gate, ff_up = [jnp.pad(w.reshape(rows, n, rows_d), ((0, 0), (0, 0), (0, spare))).reshape(rows, -1) for w in (ff_gate, ff_up)]
    fit = 128 // rows
    lane = lax.rem(me, fit) * rows
    gn = jnp.pad(jnp.stack([norm_self, norm_cross, norm_ff]).astype(F32), ((0, 5), (0, 128 - rows)))
    gn = jnp.roll(gn, lane, axis=1) if fit > 1 else gn

    back = jnp.concatenate([buckets[:1], buckets[:0:-1]])
    hot = (back[None] == jnp.arange(table.shape[0])[:, None]).astype(BF)
    taps = jnp.einsum("mh,ml->hl", table, hot, preferred_element_type=F32)[:, None]

    x = hidden_in.reshape(count * length, width)
    enc = encoded.reshape(count * keys, width)
    cot = out_cot.reshape(count * length, width)
    dseg = dec_segments.reshape(count, length)
    eseg = enc_segments.reshape(count, keys)
    weights = (self_query, self_key, self_value, self_out, cross_query, cross_out, cross_key, cross_value, ff_gate, ff_up, ff_down)
    w, out, xt, enct, hfft, hidt, dgu, r1, x1, qkv, cq, ckv, p1, p2, gain3, gains = forward(
        n, weights, gn, x, enc, cot, dseg[:, :, None], dseg[:, None, :], eseg[:, None, :], taps)
    dtok, denc, dy, dye, gain12, diag = backward(x, w, gains, r1, x1, qkv, cq, ckv, p1, p2)
    small = jnp.concatenate([gain12.reshape(-1, 128), gain3.reshape(-1, 128), diag[:, 0]])
    *parts, small = reduce_grads(n, xt, enct, hfft, hidt, dy, dye, dgu, cot, small)
    gq, gk, gv, gso, gcq, gco, gck, gcv, gg, gup, gd = finish_grads(parts)
    if spare:
        gd = gd[:rows_d]
        gg, gup = [g.reshape(rows, n, -1)[:, :, :rows_d].reshape(rows, ff) for g in (gg, gup)]
    tiles = width // 128
    flat = small[:3 * tiles].reshape(3, width)
    own = lax.dynamic_slice(flat, (0, me * rows), (3, rows))
    dtable = jnp.einsum("hl,ml->mh", small[3 * tiles:], hot.astype(F32), precision=lax.Precision.HIGHEST)
    return (
        out.reshape(hidden_in.shape), dtok.reshape(hidden_in.shape), denc.reshape(encoded.shape),
        own[0], gq, gk, gv, gso, dtable, own[1], gcq, gck, gcv, gco, own[2], gg, gup, gd,
    )


def solution(mesh):
    tok = P(None, ("shard", "rep"), None, None)
    seg = P(None, ("shard", "rep"), None)
    vec, mat, rep = P("shard"), P("shard", None), P()
    return jax.shard_map(
        functools.partial(body, n=mesh.shape["shard"]),
        mesh=mesh,
        in_specs=(tok, tok, seg, seg, rep, tok, vec, mat, mat, mat, mat, rep, vec, mat, mat, mat, mat, vec, mat, mat, mat),
        out_specs=(tok, tok, tok, vec, mat, mat, mat, mat, rep, vec, mat, mat, mat, mat, vec, mat, mat, mat),
        check_vma=False,
    )
```

time: 1710 us -> 414 us (0.24)
  waiting for transfers between devices: 1170 us -> 0 us
  Pallas kernels: 0 us -> 394 us
  matrix products: 182 us -> 2.86 us
  local copies, waits for them, and re-layouts: 158 us -> 12.4 us
  blocking collectives: 138 us -> 0 us
  other arithmetic: 36.7 us -> 3.43 us
  between operations: 17.9 us -> 0.72 us
    reduce_scatter x9 -> x0, waiting for transfers between devices: 711 us -> none  [the longest x1 129 us: body(): lax.psum_scatter(totals[12], 'shard', scatter_dimension=0, tiled=True)]
    pallas_call x0 -> x4, Pallas kernels: none -> 394 us  [the longest x1 186 us: reduce_grads(): pl.pallas_call(functools.partial(reduce_kernel, n, sizes, slots), name='r...]
    all_gather x11 -> x0, waiting for transfers between devices: 305 us -> none  [the longest x1 54.9 us: body(): lax.all_gather(ff_down, 'shard', axis=0, tiled=True)]
    dot_general x93 -> x2, matrix products: 182 us -> 2.86 us  [the longest x1 1.45 us: body(): jnp.einsum('hl,ml->mh', small[3 * tiles:], hot.astype(F32), precision=lax...]
    unnamed x25 -> x0, waiting for transfers between devices: 155 us -> none
    gather x1 -> x0, local copies, waits for them, and re-layouts: 97.2 us -> none  [body(): pair_bucket = jnp.take(buckets, distance)]
    unnamed x2 -> x0, blocking collectives: 96.2 us -> none
    psum x2 -> x0, blocking collectives: 42.1 us -> none  [the longest x1 37 us: body(): table_total = lax.psum(table_total, ('shard', 'rep'))]
  transfers between devices with their start and end apart: 23 -> 0, of which waited for: 18 -> 0; matrix products, arithmetic and copies ran while one was open for 17% -> 0% of each run, Pallas kernels for 0% -> 0%
where the time goes in v1:
time: 414 us; the launch traced here: 413 us
  Pallas kernels  394 us (95%)
  local copies, waits for them, and re-layouts  12.4 us (3%)
    pallas_call x1, Pallas kernels, reduce_grads(): pl.pallas_call(functools.partial(reduce_kernel, n, sizes, slots), name='r...  186 us
    pallas_call x1, Pallas kernels, forward(): pl.pallas_call(functools.partial(forward_kernel, n, (length, keys)), name...  160 us
    pallas_call x1, Pallas kernels, backward(): pl.pallas_call(functools.partial(backward_kernel, (length, keys)), name='...  45.8 us
    unnamed x21, local copies, waits for them, and re-layouts  8.81 us

profile of v1, /device:TPU:0, one launch (start us, length us, event | category | flops | bytes accessed | tf_op | source)
XLA Modules:
  0.0 413.1 jit_solution(8835789127062780332)
XLA Ops:
  0.7 0.7 slice.22
  1.4 0.1 rev.3
  1.5 0.7 pad_add_fusion
  2.2 0.0 copy-start.9
  2.2 0.7 fusion.13
  2.9 0.7 fusion.15.refs_11_
  3.6 0.0 copy-done.9
  3.6 1.4 fusion.1
  5.0 1.5 copy.42.refs_15_
  6.5 159.5 %gather_forward.1 = (bf16[8,1024,1024]{2,1,0:T(8,128)(2,1)}, bf16[256,1024]{1,0:T(8,128)(2,1)}, bf16[4,1024,256]{2,1,0:T(8,128)(2,1)}, bf16[1024,512]{1,0:T(8,12...) custom-call(bf16[64,1024]{1,0:T(8,128)(2,1)} %refs_0_.1, ...), custom_call_target="tpu_custom_call" | custom-call | tf_op jit(solution)/shard_map/gather_forward/pallas_call | solution.py:450
  166.0 45.8 %attention_backward.1 = (f32[256,1024]{1,0:T(8,128)}, f32[512,1024]{1,0:T(8,128)}, bf16[6,256,1024]{2,1,0:T(8,128)(2,1)}, bf16[2,512,1024]{2,1,0:T(8,128)(2,1)},...) custom-call(bf16[256,1024]{1,0:T(8,128)(2,1)} %bitcast.33, bf16[8,1024,1024]{2,1,0:T(8,128)(2,1)} %get-tuple-element.61.refs_1_, ...), custom_call_target="tpu_custom_call" | custom-call | tf_op jit(solution)/shard_map/attention_backward/pallas_call | solution.py:495
  211.8 1.3 pad_maximum_fusion.refs_8_
  213.2 186.1 %reduce_grads.1 = (bf16[6,64,1024]{2,1,0:T(8,128)(2,1)}, bf16[6,64,512]{2,1,0:T(8,128)(2,1)}, bf16[2,64,1024]{2,1,0:T(8,128)(2,1)}, bf16[2,64,512]{2,1,0:T(8,128...) custom-call(bf16[4,1024,256]{2,1,0:T(8,128)(2,1)} %get-tuple-element, ...), custom_call_target="tpu_custom_call" | custom-call | tf_op jit(solution)/shard_map/reduce_grads/pallas_call | solution.py:800
  399.3 1.5 fusion
  400.8 0.7 slice.23
  401.5 0.1 constant_dynamic-slice_fusion
  401.6 0.5 slice_bitcast_fusion
  402.1 0.0 copy-start
  402.1 1.1 copy-done
  403.2 0.0 copy-start.1
  403.2 1.1 copy-done.1
  404.3 0.0 copy-start.2
  404.3 1.0 copy-done.2
  405.3 0.0 copy-start.3
  405.3 1.0 copy-done.3
  406.3 0.0 copy-start.4
  406.3 1.0 copy-done.4
  407.3 0.0 copy-start.5
  407.3 0.9 copy-done.5
  408.3 0.0 copy-start.6
  408.3 0.9 copy-done.6
  409.2 0.0 copy-start.7
  409.2 0.9 copy-done.7
  410.1 0.0 copy-start.8
  410.1 2.2 finish_grads.1
  412.3 0.0 copy-done.8
  412.3 0.8 copy.47
  (1 shorter events, 0.0 us)
Async XLA Ops:
  2.2 1.4 copy-start.9
  402.1 1.1 copy-start
  403.2 1.1 copy-start.1
  404.3 1.0 copy-start.2
  405.3 1.0 copy-start.3
  406.3 1.0 copy-start.4
  407.3 0.9 copy-start.5
  408.3 0.9 copy-start.6
  409.2 0.9 copy-start.7
  410.1 2.2 copy-start.8

commit v2 on v1

--- a/solution.py
+++ b/solution.py
@@ -132,18 +132,32 @@
 def position_bias(taps, bias, length):
     def pair(i):
         for h in range(2):
-            w = jnp.broadcast_to(taps[2 * i + h], (length, length))
+            w = jnp.broadcast_to(taps[pl.ds(2 * i + h, 1), :], (length, length))
             bias[i, h * length:(h + 1) * length, :] = pltpu.roll(w, 0, 1, stride=1, stride_axis=0)
     each(bias.shape[0], pair)
 
 
-def seg_masks(dcol, drow, erow, neg_self, neg_cross, length):
-    for b in range(dcol.shape[0]):
-        col = dcol[b]
+def seg_masks(drow, erow, neg_self, neg_cross, length):
+    for b in range(drow.shape[0]):
+        row = drow[b].astype(F32)
+        col = jnp.broadcast_to(row, (length, length)).T
         i = lax.broadcasted_iota(jnp.int32, (length, length), 0)
         j = lax.broadcasted_iota(jnp.int32, (length, length), 1)
-        neg_self[b] = jnp.where((j <= i) & (col == drow[b]), 0.0, NEG)
-        neg_cross[b] = jnp.where(col == erow[b], 0.0, NEG)
+        neg_self[b] = jnp.where((j <= i) & (col == row), 0.0, NEG)
+        enc = erow[b].astype(F32)
+        for k in range(enc.shape[1] // length):
+            part = slice(k * length, (k + 1) * length)
+            neg_cross[b, :, part] = jnp.where(col == enc[:, part], 0.0, NEG)
+
+
+def bucket_rows(buckets, count):
+    length = buckets.shape[1]
+    i = lax.broadcasted_iota(jnp.int32, (count, length), 0)
+    hot = (i == buckets[...]).astype(F32).astype(BF)
+    m = lax.broadcasted_iota(jnp.int32, (length, length), 0)
+    l = lax.broadcasted_iota(jnp.int32, (length, length), 1)
+    back = ((m + l == length) | ((m == 0) & (l == 0))).astype(F32).astype(BF)
+    return dot(hot, back)
 
 
 def project(a, w, dst, base=None, kind=BF):
@@ -155,14 +169,14 @@
     each(dst.shape[1] // TILE, tile)
 
 
-def project_t(terms, dst, kind=F32):
+def project_t(terms, dst, kind=F32, begin=0, end=None):
     def tile(c):
         v = None
         for a, w in terms:
             u = dot_t(a[...], w[tile_at(c), :])
             v = u if v is None else v + u
         dst[:, tile_at(c)] = v.astype(kind)
-    each(dst.shape[1] // TILE, tile)
+    lax.fori_loop(begin, dst.shape[1] // TILE if end is None else end, lambda i, carry: (tile(i), carry)[1], 0)
 
 
 def feed_tile(c, h, cot, wg, wu, wd, hid, dgate, dup):
@@ -303,17 +317,26 @@
 def forward_kernel(n, dims, *refs):
     length, keys = dims
     ins, refs = refs[:11], refs[11:]
-    gn_in, x, enc, cot, dcol, drow, erow, taps = refs[:8]
-    w_out, out, xt, enct, hfft, hidt, dgu, r1, x1, qkv, cq, ckv, p1, p2, gain3, gains = refs[8:24]
-    w, gu, dn, gn, bias, neg_s, neg_c, h, hid, x2, dh, o = refs[24:36]
-    first_sems, second_sems = refs[36:46], refs[46:56]
-    load_s, store_s = refs[56:58]
+    own_gains, refs = refs[:3], refs[3:]
+    x, enc, cot, drow, erow, buckets, table = refs[:7]
+    w_out, kept, refs = refs[7], refs[8:23], refs[23:]
+    out, xt, enct, hfft, hidt, dgu, r1, x1, qkv, cq, ckv, p1, p2, gain3, gains = held = refs[:15]
+    w, gu, dn, gn, taps, bias, neg_s, neg_c, h, hid, x2, dh, o = refs[15:28]
+    first_sems, second_sems = refs[28:38], refs[38:48]
+    load_s, store_s = refs[48:50]
+
+    def stored(i):
+        return pltpu.make_async_copy(held[i], kept[i], store_s.at[i])
+
+    def store(*which):
+        for i in which:
+            stored(i).start()
     geo = geometry(n)
     chips, me, rep, core, ring, device_at = geo
     hops = chips - 1
     rows, rows_d = ins[0].shape[0], ins[10].shape[0]
     half, half_g = w.shape[2] // 2, gu.shape[2] // 2
-    count = dcol.shape[0]
+    count = drow.shape[0]
     pairs = w.shape[2] // 128
 
     def block(src):
@@ -334,22 +357,30 @@
     first = Gather(geo, attention_pieces, 2, first_sems)
     second = Gather(geo, feed_pieces, 1, second_sems)
 
+    width = w.shape[2]
     places = [w.at[i, block(me), :] for i in range(8)] + [gu.at[i, block(me), :] for i in range(2)] + [dn.at[block_d(me), :]]
-    loads = [pltpu.make_async_copy(a, b, load_s.at[i]) for i, (a, b) in enumerate(zip(ins + (gn_in,), places + [gn.at[me]]))]
+    loads = [pltpu.make_async_copy(a, b, load_s.at[i]) for i, (a, b) in enumerate(zip(ins, places))]
     for c in loads:
         c.start()
     barrier = pltpu.get_barrier_semaphore()
     for dev in first.ahead + (first.sibling, first.opposite):
         pl.semaphore_signal(barrier, inc=1, device_id=dev, device_id_type=MESH)
+    per = 128 // rows
+    lane = lax.broadcasted_iota(jnp.int32, (rows, 128), 1)
+    spot = lax.broadcasted_iota(jnp.int32, (rows, 128), 0)
+    place = (lane == spot + lax.rem(me, per) * rows).astype(F32).astype(BF)
+    gn[me] = jnp.concatenate([dot(g[...], place) for g in own_gains] + [jnp.zeros((5, 128), F32)], axis=0)
     for c in loads:
         c.wait()
     pl.semaphore_wait(barrier, 4)
 
     first.start()
     turn(enc, enct)
+    store(2)
     first.hop(0)
+    taps[...] = dot(table[...], bucket_rows(buckets, table.shape[1]).astype(BF))
     position_bias(taps, bias, length)
-    seg_masks(dcol, drow, erow, neg_s, neg_c, length)
+    seg_masks(drow, erow, neg_s, neg_c, length)
 
     def middle(t):
         first.hop(t)
@@ -360,16 +391,15 @@
     first.relay(hops - 2)
     first.relay(hops - 1)
     first.complete()
-    store = pltpu.make_async_copy(w, w_out, store_s)
-    store.start()
-
-    per = 128 // rows
+    weights_out = pltpu.make_async_copy(w, w_out, store_s.at[15])
+    weights_out.start()
     for j in range(w.shape[2] // 128):
         v = gn[j * per]
         for i in range(1, per):
             v = v + gn[j * per + i]
         for i in range(3):
             gains[i, :, j * 128:(j + 1) * 128] = v[i:i + 1, :]
+    store(14)
 
     def some(begin, end, f):
         lax.fori_loop(begin, end, lambda i, c: (f(i), c)[1], 0)
@@ -383,6 +413,7 @@
         attend(i, qkv.at[0], qkv.at[1], qkv.at[2], p1, o, neg_s, bias, length, length)
 
     def cross_heads():
+        store(8, 11)
         turn(h, xt.at[0])
         turn(o, xt.at[1])
         project(o, w.at[3], x1, base=x, kind=F32)
@@ -390,6 +421,7 @@
         project(h, w.at[4], cq)
 
     def cross_keys():
+        store(7, 9)
         turn(h, xt.at[2])
         for i in range(2):
             project(enc, w.at[6 + i], ckv.at[i])
@@ -398,10 +430,13 @@
         attend(i, cq, ckv.at[0], ckv.at[1], p2, o, neg_c, None, length, keys)
 
     def before_feed():
+        store(10, 12)
         turn(o, xt.at[3])
+        store(1)
         project(o, w.at[5], x2, base=x1, kind=F32)
         normed(x2, gains.at[2], h)
         turn(h, hfft)
+        store(3)
 
     total = count * pairs
     mid = total // 2
@@ -424,21 +459,27 @@
     second.complete()
 
     each(hid.shape[1] // TILE, lambda c: feed_tile(c, h, cot, gu.at[0], gu.at[1], dn, hid, dgu.at[0], dgu.at[1]))
+    store(5)
+    turn(hid, hidt)
+    store(4)
     project_t([(dgu.at[0], gu.at[0]), (dgu.at[1], gu.at[1])], dh)
     norm_back(x2, gains.at[2], dh, cot, r1, gain3)
+    store(6, 13)
     project(hid, dn, out, base=x2)
-    turn(hid, hidt)
+    store(0)
     first.drain()
     second.drain()
-    store.wait()
-
-
-def forward(n, weights, gn, x, enc, cot, dcol, drow, erow, taps):
+    weights_out.wait()
+    for i in range(15):
+        stored(i).wait()
+
+
+def forward(n, weights, own_gains, x, enc, cot, drow, erow, buckets, table):
     hops = n // 2 - 1
     rows, width = weights[0].shape
     ff = weights[8].shape[1]
     tokens, etokens = x.shape[0], enc.shape[0]
-    count, length, _ = dcol.shape
+    count, _, length = drow.shape
     keys = etokens // count
     pairs = width // 128
     S = jax.ShapeDtypeStruct
@@ -446,62 +487,27 @@
     def v(*shape, t=BF):
         return pltpu.VMEM(shape, t)
 
+    kept = [
+        S((tokens, width), BF), S((4, width, tokens), BF), S((width, etokens), BF),
+        S((width, tokens), BF), S((ff, tokens), BF), S((2, tokens, ff), BF), S((tokens, width), F32), S((tokens, width), F32),
+        S((3, tokens, width), BF), S((tokens, width), BF), S((2, etokens, width), BF),
+        S((count * pairs, 2 * length, length), BF), S((count * pairs, 2 * length, keys), BF),
+        S((1, width), F32), S((3, 1, width), F32),
+    ]
     vm, hbm = pl.BlockSpec(memory_space=pltpu.VMEM), pl.BlockSpec(memory_space=pl.ANY)
     return pl.pallas_call(
         functools.partial(forward_kernel, n, (length, keys)),
         name="gather_forward",
-        out_shape=(
-            S((8, width, width), BF), S((tokens, width), BF), S((4, width, tokens), BF), S((width, etokens), BF),
-            S((width, tokens), BF), S((ff, tokens), BF), S((2, tokens, ff), BF), S((tokens, width), F32), S((tokens, width), F32),
-            S((3, tokens, width), BF), S((tokens, width), BF), S((2, etokens, width), BF),
-            S((count * pairs, 2 * length, length), BF), S((count * pairs, 2 * length, keys), BF),
-            S((1, width), F32), S((3, 1, width), F32),
-        ),
-        in_specs=[hbm] * 12 + [vm] * 7,
-        out_specs=[hbm] + [vm] * 15,
-        scratch_shapes=[
-            v(8, width, width), v(2, width, ff), v(ff, width), v(n, 8, 128, t=F32),
+        out_shape=(S((8, width, width), BF),) + tuple(kept),
+        in_specs=[hbm] * 11 + [vm] * 10,
+        out_specs=[hbm] * 16,
+        scratch_shapes=[v(*a.shape, t=a.dtype) for a in kept] + [
+            v(8, width, width), v(2, width, ff), v(ff, width), v(n, 8, 128, t=F32), v(table.shape[0], length, t=F32),
             v(pairs, 2 * length, length, t=F32), v(count, length, length, t=F32), v(count, length, keys, t=F32),
             v(tokens, width), v(tokens, ff), v(tokens, width, t=F32), v(tokens, width, t=F32), v(tokens, width),
-        ] + gather_sems(hops, 5, 2) + gather_sems(hops, 2, 1) + [pltpu.SemaphoreType.DMA((12,)), pltpu.SemaphoreType.DMA(())],
+        ] + gather_sems(hops, 5, 2) + gather_sems(hops, 2, 1) + [pltpu.SemaphoreType.DMA((11,)), pltpu.SemaphoreType.DMA((16,))],
         compiler_params=pltpu.CompilerParams(collective_id=0, has_side_effects=True, vmem_limit_bytes=67043328),
-    )(*weights, gn, x, enc, cot, dcol, drow, erow, taps)
-
-
-def backward_kernel(dims, *refs):
-    length, keys = dims
-    x, w, gains, r1, x1, qkv, cq, ckv, p1, p2, dtok, denc, dy, dye, gain12, diag, dh, r0, do = refs
-    diag[...] = jnp.zeros(diag.shape, F32)
-    total = p1.shape[0]
-    dy[5] = r1[...].astype(BF)
-    project_t([(dy.at[5], w.at[5])], do, kind=BF)
-    each(total, lambda i: attend_back(i, cq, ckv.at[0], ckv.at[1], p2, do, dy.at[4], dye.at[0], dye.at[1], None, length, keys))
-    project_t([(dye.at[0], w.at[6]), (dye.at[1], w.at[7])], denc)
-    project_t([(dy.at[4], w.at[4])], dh)
-    norm_back(x1, gains.at[1], dh, r1, r0, gain12.at[1])
-    dy[3] = r0[...].astype(BF)
-    project_t([(dy.at[3], w.at[3])], do, kind=BF)
-    each(total, lambda i: attend_back(i, qkv.at[0], qkv.at[1], qkv.at[2], p1, do, dy.at[0], dy.at[1], dy.at[2], diag, length, length))
-    project_t([(dy.at[0], w.at[0]), (dy.at[1], w.at[1]), (dy.at[2], w.at[2])], dh)
-    norm_back(x, gains.at[0], dh, r0, dtok, gain12.at[0])
-
-
-def backward(x, w, gains, r1, x1, qkv, cq, ckv, p1, p2):
-    tokens, width = x.shape
-    etokens = ckv.shape[1]
-    length, keys = p1.shape[2], p2.shape[2]
-    S = jax.ShapeDtypeStruct
-    vm = pl.BlockSpec(memory_space=pltpu.VMEM)
-    return pl.pallas_call(
-        functools.partial(backward_kernel, (length, keys)),
-        name="attention_backward",
-        out_shape=(S((tokens, width), F32), S((etokens, width), F32), S((6, tokens, width), BF), S((2, etokens, width), BF),
-                   S((2, 1, width), F32), S((width // 64, 1, 128), F32)),
-        in_specs=[vm] * 10,
-        out_specs=[vm] * 6,
-        scratch_shapes=[pltpu.VMEM((tokens, width), F32), pltpu.VMEM((tokens, width), F32), pltpu.VMEM((tokens, width), BF)],
-        compiler_params=pltpu.CompilerParams(vmem_limit_bytes=67043328),
-    )(x, w, gains, r1, x1, qkv, cq, ckv, p1, p2)
+    )(*weights, *own_gains, x, enc, cot, drow, erow, buckets, table)
 
 
 class Group:
@@ -643,6 +649,16 @@
                     if k == 0:
                         self.claim(2, t + 1, way)
                     self.ring_copies(t, way)[k].start()
+
+                @pl.when(t == self.chips - 1)
+                def _():
+                    for c in self.final_copies(way, k):
+                        c.start()
+                    last = (self.chips - 1) % 2
+                    cols = pl.ds(pl.multiple_of(way * g.half + self.rep * g.share, 128), g.share)
+                    g.own[:, :, cols] = g.rs[last, way, :, :, :g.share]
+                    rest = pl.ds(pl.multiple_of(way * g.half + 2 * g.share, 128), g.half - 2 * g.share)
+                    g.own[:, :, rest] = g.rs[last, way, :, :, g.share:]
                 if k == len(self.groups) - 1:
                     self.release(0, t, way, self.sibling)
                     self.release(1, t, way, self.opposite)
@@ -653,46 +669,38 @@
         for g in self.groups:
             g.rr[0] = jnp.zeros(g.rr.shape[1:], BF)
 
-    def final_copies(self):
-        s = (self.chips - 1) % 2
-        found = []
-        for way in range(2):
-            for i, g in enumerate(self.groups):
-                mine = g.rs.at[s, way]
-                cols = pl.ds(pl.multiple_of(way * g.half + self.rep * g.share, 128), g.share)
-                wide = g.half - 2 * g.share
-                found.append(rdma(mine.at[:, :, pl.ds(0, g.share)], g.own.at[:, :, cols],
-                                  self.fin_s.at[way, 2 * i], self.fin_r.at[way, 2 * i], self.opposite))
-                found.append(rdma(mine.at[:, :, pl.ds(g.share, wide)], g.got.at[:, :, pl.ds(way * wide, wide)],
-                                  self.fin_s.at[way, 2 * i + 1], self.fin_r.at[way, 2 * i + 1], self.opposite))
-        return found
-
-    def send_finals(self):
-        s = (self.chips - 1) % 2
-        for c in self.final_copies():
-            c.start()
-        for way in range(2):
-            for g in self.groups:
-                cols = pl.ds(pl.multiple_of(way * g.half + self.rep * g.share, 128), g.share)
-                g.own[:, :, cols] = g.rs[s, way, :, :, :g.share]
-                g.own[:, :, way * g.half + 2 * g.share:(way + 1) * g.half] = g.rs[s, way, :, :, g.share:]
+    def final_copies(self, way, k):
+        g = self.groups[k]
+        mine = g.rs.at[(self.chips - 1) % 2, way]
+        cols = pl.ds(pl.multiple_of(way * g.half + self.rep * g.share, 128), g.share)
+        wide = g.half - 2 * g.share
+        there = pl.ds(pl.multiple_of(way * wide, 128), wide)
+        return [rdma(mine.at[:, :, pl.ds(0, g.share)], g.own.at[:, :, cols],
+                     self.fin_s.at[way, 2 * k], self.fin_r.at[way, 2 * k], self.opposite),
+                rdma(mine.at[:, :, pl.ds(g.share, wide)], g.got.at[:, :, there],
+                     self.fin_s.at[way, 2 * k + 1], self.fin_r.at[way, 2 * k + 1], self.opposite)]
 
     def finish(self):
-        for way in range(2):
-            for i, g in enumerate(self.groups):
+        def go(way):
+            for k, g in enumerate(self.groups):
                 wide = g.half - 2 * g.share
                 ref = g.own.at[:, :, pl.ds(pl.multiple_of(way * g.half + self.other * g.share, 128), g.share)]
-                rdma(ref, ref, self.fin_s.at[way, 2 * i], self.fin_r.at[way, 2 * i], self.opposite).wait_recv()
-                ref = g.got.at[:, :, pl.ds(way * wide, wide)]
-                rdma(ref, ref, self.fin_s.at[way, 2 * i + 1], self.fin_r.at[way, 2 * i + 1], self.opposite).wait_recv()
-        for c in self.final_copies():
-            c.wait_send()
-        for way in range(2):
+                rdma(ref, ref, self.fin_s.at[way, 2 * k], self.fin_r.at[way, 2 * k], self.opposite).wait_recv()
+                ref = g.got.at[:, :, pl.ds(pl.multiple_of(way * wide, 128), wide)]
+                rdma(ref, ref, self.fin_s.at[way, 2 * k + 1], self.fin_r.at[way, 2 * k + 1], self.opposite).wait_recv()
+                for c in self.final_copies(way, k):
+                    c.wait_send()
             for t in (self.chips - 2, self.chips - 1):
                 for c in self.sib_copies(t, way) + self.y_copies(t, way):
                     c.wait_send()
             for c in self.ring_copies(self.chips - 2, way):
                 c.wait_send()
+        each(2, go)
+
+    def at(self, t, f):
+        @pl.when((t >= 0) & (t < self.chips))
+        def _():
+            f(t)
 
 
 class Butterfly:
@@ -723,123 +731,259 @@
             self.copy(j, self.partner(1)).wait_send()
 
 
-def reduce_kernel(n, sizes, slots, *refs):
-    xt, enct, hfft, hidt, dy, dye, dgu, cot, small = refs[:9]
-    outs, small_o = refs[9:17], refs[17]
-    bufs, sems = refs[18:42], refs[42:51]
-    sm, sm_got, sm_s, sm_r = refs[51:]
+OFFSETS = (0, 0, 0, 5, 8)
+CHAINS = ((2,), (3,), (4,), (0, 5), (1,))
+SLOTS = (3, 3, 3)
+
+
+def backward_kernel(n, sizes, dims, *refs):
+    length, keys = dims
+    ins, w_hbm, refs = refs[:16], refs[16], refs[17:]
+    outs, (small_o, dtok, denc), refs = refs[:12], refs[12:15], refs[15:]
+    held, refs = refs[:16], refs[16:]
+    hfft, hidt, dgu, cot, r1, cq, ckv, p2, x1, gains, qkv, p1, x, xt, enct, gain3 = held
+    bufs, refs = refs[:36], refs[36:]
+    sems, refs = [refs[9 * k:9 * k + 9] for k in range(5)], refs[45:]
+    sm, sm_got, sm_s, sm_r, load_s, w, w_s, dy, dye, dh, r0, do, gain12, diag = refs
     geo = geometry(n)
     chips, me, rep, core, ring, device_at = geo
-    rows, rows_d = sizes[0][1], sizes[3][1]
-    which = (0, 0, 0, 1, 2, 3)
+    rows, rows_d = sizes[0][1], sizes[4][1]
+
+    loads = [pltpu.make_async_copy(a, b, load_s.at[i]) for i, (a, b) in enumerate(zip(ins, held))]
+    for c in loads:
+        c.start()
+
+    def fetch(i, slot):
+        return pltpu.make_async_copy(w_hbm.at[i], w.at[slot], w_s.at[slot])
+    for i, slot in ((5, 0), (6, 1), (7, 2), (4, 3)):
+        fetch(i, slot).start()
 
     def block(dev, size):
         return pl.ds(pl.multiple_of(dev * size, size), size)
-    lefts = [lambda i, dev: xt[which[i], block(dev, rows), :], lambda i, dev: enct[block(dev, rows), :],
-             lambda i, dev: hfft[block(dev, rows), :], lambda i, dev: hidt[block(dev, rows_d), :]]
-    rights = [lambda i, c: dy[i, :, c], lambda i, c: dye[i, :, c], lambda i, c: dgu[i, :, c], lambda i, c: cot[:, c]]
-    groups = [Group(lefts[k], rights[k], sizes[k], bufs[6 * k:6 * k + 6] + outs[2 * k:2 * k + 2]) for k in range(4)]
-    red = Reduce(geo, groups, slots, sems)
+    lefts = [lambda i, dev: xt[(3, 2)[i], block(dev, rows), :], lambda i, dev: xt[(1, 0, 0, 0)[i], block(dev, rows), :],
+             lambda i, dev: hfft[block(dev, rows), :], lambda i, dev: hfft[block(dev, rows), :],
+             lambda i, dev: hidt[block(dev, rows_d), :], lambda i, dev: enct[block(dev, rows), :]]
+    rights = [lambda i, c: dy[i, :, c], lambda i, c: dy[2 + i, :, c], lambda i, c: dgu[0, :, c], lambda i, c: dgu[1, :, c],
+              lambda i, c: cot[:, c], lambda i, c: dye[i, :, c]]
+    groups = [Group(lefts[k], rights[k], sizes[k], bufs[6 * k:6 * k + 6] + outs[2 * k:2 * k + 2]) for k in range(6)]
+    chains = [Reduce(geo, [groups[k] for k in c], SLOTS, s) for c, s in zip(CHAINS, sems)]
     tree = Butterfly(geo, n, sm, sm_got, (sm_s, sm_r))
+    lead = chains[0]
 
     barrier = pltpu.get_barrier_semaphore()
-    greet = [red.after[0], red.after[1], red.sibling, red.opposite] + [tree.partner(1 << j) for j in range(tree.stages)]
+    greet = [lead.after[0], lead.after[1], lead.sibling, lead.opposite] + [tree.partner(1 << j) for j in range(tree.stages)]
     for dev in greet:
         pl.semaphore_signal(barrier, inc=1, device_id=dev, device_id_type=MESH)
+    for g in groups:
+        g.rr[0] = jnp.zeros(g.rr.shape[1:], BF)
+    diag[...] = jnp.zeros(diag.shape, F32)
+    for c in loads[:4]:
+        c.wait()
     pl.semaphore_wait(barrier, len(greet))
 
-    red.prepare()
-    sm[0] = small[...]
-    tree.begin()
-    red.to_sibling(0)
-    red.to_sibling(1)
-    red.to_across(0)
-    red.to_sibling(2)
-    red.to_across(1)
-
-    def step(t, bit):
-        red.to_ring(t)
-
-        @pl.when(t + 2 < chips)
+    total = p1.shape[0]
+    width = dh.shape[1]
+
+    def start_back():
+        for c in loads[4:]:
+            c.wait()
+        dy[0] = r1[...].astype(BF)
+        fetch(5, 0).wait()
+        project_t([(dy.at[0], w.at[0])], do, kind=BF)
+        fetch(3, 0).start()
+
+    def cross(begin, end):
+        def f():
+            lax.fori_loop(begin, end, lambda i, c: (attend_back(
+                i, cq, ckv.at[0], ckv.at[1], p2, do, dy.at[1], dye.at[0], dye.at[1], None, length, keys), c)[1], 0)
+        return f
+
+    def own(begin, end):
+        def f():
+            lax.fori_loop(begin, end, lambda i, c: (attend_back(
+                i, qkv.at[0], qkv.at[1], qkv.at[2], p1, do, dy.at[3], dy.at[4], dy.at[5], diag, length, length), c)[1], 0)
+        return f
+
+    def encoder(begin, end, last):
+        def f():
+            if not last:
+                fetch(6, 1).wait()
+                fetch(7, 2).wait()
+            project_t([(dye.at[0], w.at[1]), (dye.at[1], w.at[2])], denc, begin=begin, end=end)
+            if last:
+                fetch(0, 1).start()
+                fetch(1, 2).start()
+        return f
+
+    def cross_norm():
+        norm_back(x1, gains.at[1], dh, r1, r0, gain12.at[1])
+        dy[2] = r0[...].astype(BF)
+
+    def cross_query():
+        fetch(4, 3).wait()
+        project_t([(dy.at[1], w.at[3])], dh)
+        fetch(2, 3).start()
+
+    def own_out():
+        fetch(3, 0).wait()
+        project_t([(dy.at[2], w.at[0])], do, kind=BF)
+
+    def own_in(begin, end, last):
+        def f():
+            if not last:
+                for i, slot in ((0, 1), (1, 2), (2, 3)):
+                    fetch(i, slot).wait()
+            project_t([(dy.at[3], w.at[1]), (dy.at[4], w.at[2]), (dy.at[5], w.at[3])], dh, begin=begin, end=end)
+        return f
+
+    def own_norm():
+        norm_back(x, gains.at[0], dh, r0, dtok, gain12.at[0])
+        for k in range(width // 128):
+            for i, g in enumerate((gain12.at[0], gain12.at[1], gain3)):
+                sm[0, pl.ds(i * (width // 128) + k, 1), :] = g[:, k * 128:(k + 1) * 128]
+        for i in range(diag.shape[0]):
+            sm[0, pl.ds(3 * (width // 128) + i, 1), :] = diag[i]
+
+    tiles = width // TILE
+    pieces = [start_back]
+    pieces += [cross(total * k // 8, total * (k + 1) // 8) for k in range(8)]
+    pieces += [cross_query, cross_norm, own_out]
+    pieces += [own(total * k // 5, total * (k + 1) // 5) for k in range(5)]
+    pieces += [encoder(0, tiles // 2, False), encoder(tiles // 2, tiles, True)]
+    pieces += [own_in(0, tiles // 2, False), own_in(tiles // 2, tiles, True), own_norm]
+    tree_at = 7
+
+    def piece(u, which):
+        for i in range(which, len(pieces), 3):
+            pl.when(u == i // 3)(pieces[i])
+
+    def step(v, bit):
+        u = v - 3
+        for k, c in enumerate(chains):
+            c.at(u - OFFSETS[k], c.to_ring)
+            if k < 3:
+                piece(u, k)
+        for k, c in enumerate(chains):
+            c.at(u - OFFSETS[k] + 2, c.to_across)
+        for k, c in enumerate(chains):
+            c.at(u - OFFSETS[k] + 3, c.to_sibling)
+        pl.when(u == tree_at)(tree.begin)
+        inside = (u > tree_at) & (u <= tree_at + tree.stages)
+
+        @pl.when(inside)
         def _():
-            red.to_across(t + 2)
-
-        @pl.when(t + 3 < chips)
-        def _():
-            red.to_sibling(t + 3)
-
-        @pl.when(t < tree.stages)
-        def _():
-            tree.stage(t + 1, bit)
-        return bit * 2
-
-    lax.fori_loop(0, chips, step, 1)
-    red.send_finals()
+            tree.stage(u - tree_at, bit)
+        return jnp.where(inside, bit * 2, bit)
+
+    lax.fori_loop(0, OFFSETS[-1] + chips + 3, step, jnp.int32(1))
     tree.end(small_o)
-    red.finish()
+    for c in chains:
+        c.finish()
 
 
 def shares(half):
     return max(1, half // 512) * 128
 
 
-def reduce_grads(n, xt, enct, hfft, hidt, dy, dye, dgu, cot, small):
+def backward(n, w, hfft, hidt, dgu, cot, r1, cq, ckv, p2, x1, gains, qkv, p1, x, xt, enct, gain3):
     chips = n // 2
-    width, ff = dy.shape[2], dgu.shape[2]
+    tokens, width = x.shape
+    etokens, ff = enct.shape[1], dgu.shape[2]
+    length, keys = p1.shape[2], p2.shape[2]
     rows, rows_d = width // n, hidt.shape[0] // n
-    sizes = [(6, rows, width // 2, shares(width // 2)), (2, rows, width // 2, shares(width // 2)),
-             (2, rows, ff // 2, shares(ff // 2)), (1, rows_d, width // 2, shares(width // 2))]
-    slots = (chips, chips, chips)
+    half, half_g = width // 2, ff // 2
+    sizes = [(2, rows, half, shares(half)), (4, rows, half, shares(half)), (1, rows, half_g, shares(half_g)),
+             (1, rows, half_g, shares(half_g)), (1, rows_d, half, shares(half)), (2, rows, half, shares(half))]
     stages = n.bit_length() - 1
     dma = pltpu.SemaphoreType.DMA
     S = jax.ShapeDtypeStruct
-    vm = pl.BlockSpec(memory_space=pltpu.VMEM)
+    vm, hbm = pl.BlockSpec(memory_space=pltpu.VMEM), pl.BlockSpec(memory_space=pl.ANY)
     outs = []
-    for count, r, half, share in sizes:
-        outs += [S((count, r, 2 * half), BF), S((count, r, 2 * (half - 2 * share)), BF)]
+    for count, r, h, share in sizes:
+        outs += [S((count, r, 2 * h), BF), S((count, r, 2 * (h - 2 * share)), BF)]
+    small = (3 * (width // 128) + width // 64, 128)
+    ins = (hfft, hidt, dgu, cot, r1, cq, ckv, p2, x1, gains, qkv, p1, x, xt, enct, gain3)
+    slots = tuple(min(s, chips) for s in SLOTS)
     return pl.pallas_call(
-        functools.partial(reduce_kernel, n, sizes, slots),
-        name="reduce_grads",
-        out_shape=tuple(outs) + (S(small.shape, F32),),
-        in_specs=[vm] * 9,
-        out_specs=[vm] * 9,
-        scratch_shapes=[b for size in sizes for b in group_shapes(size, slots)] + reduce_sems(4, slots)
-        + [pltpu.VMEM((stages + 1,) + small.shape, F32)] * 2 + [dma((stages + 1,))] * 2,
+        functools.partial(backward_kernel, n, sizes, (length, keys)),
+        name="backward_reduce",
+        out_shape=tuple(outs) + (S(small, F32), S((tokens, width), F32), S((etokens, width), F32)),
+        in_specs=[hbm] * 17,
+        out_specs=[vm] * 15,
+        scratch_shapes=[pltpu.VMEM(a.shape, a.dtype) for a in ins]
+        + [b for size in sizes for b in group_shapes(size, slots)]
+        + [s for c in CHAINS for s in reduce_sems(len(c), slots)]
+        + [pltpu.VMEM((stages + 1,) + small, F32)] * 2 + [dma((stages + 1,))] * 2
+        + [dma((16,)), pltpu.VMEM((4, width, width), BF), dma((4,)), pltpu.VMEM((6, tokens, width), BF),
+           pltpu.VMEM((2, etokens, width), BF), pltpu.VMEM((tokens, width), F32), pltpu.VMEM((tokens, width), F32),
+           pltpu.VMEM((tokens, width), BF), pltpu.VMEM((2, 1, width), F32), pltpu.VMEM((width // 64, 1, 128), F32)],
         compiler_params=pltpu.CompilerParams(collective_id=1, has_side_effects=True, vmem_limit_bytes=67043328),
-    )(xt, enct, hfft, hidt, dy, dye, dgu, cot, small)
-
-
-def finish_kernel(sizes, *refs):
-    at = 8
+    )(*ins, w)
+
+
+def finish_kernel(sizes, passed, buckets_count, *refs):
+    parts, mats = 2 * len(sizes), sum(s[0] for s in sizes)
+    ins, (small, buckets), refs = refs[:parts + passed], refs[parts + passed:parts + passed + 2], refs[parts + passed + 2:]
+    outs, (dtable, gain1, gain2, gain3), refs = refs[:mats + passed], refs[mats + passed:mats + passed + 4], refs[mats + passed + 4:]
+    held, done, (load_s, store_s) = refs[:parts + passed], refs[parts + passed:-2], refs[-2:]
+    loads = [pltpu.make_async_copy(a, b, load_s.at[i]) for i, (a, b) in enumerate(zip(ins, held))]
+    stores = [pltpu.make_async_copy(a, b, store_s.at[i]) for i, (a, b) in enumerate(zip(done + held[parts:], outs))]
+    for c in loads:
+        c.start()
+    at = 0
     for k, (count, rows, half, share) in enumerate(sizes):
-        own, got = refs[2 * k], refs[2 * k + 1]
+        own, got = held[2 * k], held[2 * k + 1]
+        loads[2 * k].wait()
+        loads[2 * k + 1].wait()
         wide = half - 2 * share
         for i in range(count):
-            dst = refs[at]
-            at += 1
             for way in range(2):
                 lo = way * half
-                dst[:, lo:lo + 2 * share] = own[i, :, lo:lo + 2 * share].astype(F32)
+                done[at][:, lo:lo + 2 * share] = own[i, :, lo:lo + 2 * share].astype(F32)
                 v = own[i, :, lo + 2 * share:lo + half].astype(F32) + got[i, :, way * wide:(way + 1) * wide].astype(F32)
-                dst[:, lo + 2 * share:lo + half] = v
-
-
-def finish_grads(parts):
+                done[at][:, lo + 2 * share:lo + half] = v
+            stores[at].start()
+            at += 1
+    for i in range(passed):
+        loads[parts + i].wait()
+        stores[mats + i].start()
+    me = lax.axis_index("shard")
+    rows = gain1.shape[1]
+    per = 128 // rows
+    heads = dtable.shape[0]
+    tiles = (small.shape[0] - heads) // 3
+    tile = lax.broadcasted_iota(jnp.int32, (tiles, 128), 0)
+    for i, dst in enumerate((gain1, gain2, gain3)):
+        v = jnp.where(tile == lax.div(me, per), small[i * tiles:(i + 1) * tiles, :], 0.0)
+        v = pltpu.roll(v, lax.rem(128 - lax.rem(me, per) * rows, 128), 1)
+        dst[...] = jnp.sum(v, axis=0, keepdims=True)[:, :rows]
+    dtable[...] = lax.dot_general(small[3 * tiles:, :], bucket_rows(buckets, buckets_count), (((1,), (1,)), ((), ())),
+                                  precision=lax.Precision.HIGHEST, preferred_element_type=F32)
+    for c in stores:
+        c.wait()
+
+
+def finish(parts, passed, small, buckets, shape, rows):
     sizes, outs = [], []
+    S = jax.ShapeDtypeStruct
     for own, got in zip(parts[0::2], parts[1::2]):
-        count, rows, width = own.shape
+        count, r, width = own.shape
         half = width // 2
-        sizes.append((count, rows, half, (half - got.shape[2] // 2) // 2))
-        outs += [jax.ShapeDtypeStruct((rows, width), F32)] * count
-    vm = pl.BlockSpec(memory_space=pltpu.VMEM)
+        sizes.append((count, r, half, (half - got.shape[2] // 2) // 2))
+        outs += [S((r, width), F32)] * count
+    vm, hbm = pl.BlockSpec(memory_space=pltpu.VMEM), pl.BlockSpec(memory_space=pl.ANY)
+    ins = list(parts) + list(passed)
+    dma = pltpu.SemaphoreType.DMA
     return pl.pallas_call(
-        functools.partial(finish_kernel, sizes),
-        name="finish_grads",
-        out_shape=tuple(outs),
-        in_specs=[vm] * len(parts),
-        out_specs=[vm] * len(outs),
-        compiler_params=pltpu.CompilerParams(vmem_limit_bytes=40 << 20),
-    )(*parts)
+        functools.partial(finish_kernel, sizes, len(passed), shape[1]),
+        name="finish",
+        out_shape=tuple(outs) + tuple(S(a.shape, a.dtype) for a in passed) + (S(shape, F32),) + (S((1, rows), F32),) * 3,
+        in_specs=[hbm] * len(ins) + [vm] * 2,
+        out_specs=[hbm] * (len(outs) + len(passed)) + [vm] * 4,
+        scratch_shapes=[pltpu.VMEM(a.shape, a.dtype) for a in ins] + [pltpu.VMEM(a.shape, a.dtype) for a in outs]
+        + [dma((len(ins),)), dma((len(outs) + len(passed),))],
+        compiler_params=pltpu.CompilerParams(vmem_limit_bytes=67043328),
+    )(*ins, small, buckets)
 
 
 def body(hidden_in, encoded, dec_segments, enc_segments, buckets, out_cot, norm_self, self_query, self_key, self_value,
@@ -848,42 +992,27 @@
     keys = encoded.shape[2]
     count = micro * per
     rows, rows_d, ff = self_query.shape[0], ff_down.shape[0], ff_gate.shape[1]
-    me = lax.axis_index("shard")
     spare = -rows_d % 16
     if spare:
         ff_down = jnp.pad(ff_down, ((0, spare), (0, 0)))
         ff_gate, ff_up = [jnp.pad(w.reshape(rows, n, rows_d), ((0, 0), (0, 0), (0, spare))).reshape(rows, -1) for w in (ff_gate, ff_up)]
-    fit = 128 // rows
-    lane = lax.rem(me, fit) * rows
-    gn = jnp.pad(jnp.stack([norm_self, norm_cross, norm_ff]).astype(F32), ((0, 5), (0, 128 - rows)))
-    gn = jnp.roll(gn, lane, axis=1) if fit > 1 else gn
-
-    back = jnp.concatenate([buckets[:1], buckets[:0:-1]])
-    hot = (back[None] == jnp.arange(table.shape[0])[:, None]).astype(BF)
-    taps = jnp.einsum("mh,ml->hl", table, hot, preferred_element_type=F32)[:, None]
-
     x = hidden_in.reshape(count * length, width)
     enc = encoded.reshape(count * keys, width)
     cot = out_cot.reshape(count * length, width)
-    dseg = dec_segments.reshape(count, length)
-    eseg = enc_segments.reshape(count, keys)
+    buckets = buckets.reshape(1, length)
     weights = (self_query, self_key, self_value, self_out, cross_query, cross_out, cross_key, cross_value, ff_gate, ff_up, ff_down)
+    own_gains = [g.reshape(1, rows) for g in (norm_self, norm_cross, norm_ff)]
     w, out, xt, enct, hfft, hidt, dgu, r1, x1, qkv, cq, ckv, p1, p2, gain3, gains = forward(
-        n, weights, gn, x, enc, cot, dseg[:, :, None], dseg[:, None, :], eseg[:, None, :], taps)
-    dtok, denc, dy, dye, gain12, diag = backward(x, w, gains, r1, x1, qkv, cq, ckv, p1, p2)
-    small = jnp.concatenate([gain12.reshape(-1, 128), gain3.reshape(-1, 128), diag[:, 0]])
-    *parts, small = reduce_grads(n, xt, enct, hfft, hidt, dy, dye, dgu, cot, small)
-    gq, gk, gv, gso, gcq, gco, gck, gcv, gg, gup, gd = finish_grads(parts)
+        n, weights, own_gains, x, enc, cot, dec_segments.reshape(count, 1, length), enc_segments.reshape(count, 1, keys), buckets, table.T)
+    *parts, small, dtok, denc = backward(n, w, hfft, hidt, dgu, cot, r1, cq, ckv, p2, x1, gains, qkv, p1, x, xt, enct, gain3)
+    gco, gcq, gso, gq, gk, gv, gg, gup, gd, gck, gcv, out, dtok, denc, dtable, g1, g2, g3 = finish(
+        parts, (out, dtok, denc), small, buckets, table.T.shape, rows)
     if spare:
         gd = gd[:rows_d]
         gg, gup = [g.reshape(rows, n, -1)[:, :, :rows_d].reshape(rows, ff) for g in (gg, gup)]
-    tiles = width // 128
-    flat = small[:3 * tiles].reshape(3, width)
-    own = lax.dynamic_slice(flat, (0, me * rows), (3, rows))
-    dtable = jnp.einsum("hl,ml->mh", small[3 * tiles:], hot.astype(F32), precision=lax.Precision.HIGHEST)
     return (
         out.reshape(hidden_in.shape), dtok.reshape(hidden_in.shape), denc.reshape(encoded.shape),
-        own[0], gq, gk, gv, gso, dtable, own[1], gcq, gck, gcv, gco, own[2], gg, gup, gd,
+        g1.reshape(rows), gq, gk, gv, gso, dtable.T, g2.reshape(rows), gcq, gck, gcv, gco, g3.reshape(rows), gg, gup, gd,
     )
 
 

time: 414 us -> 333 us (0.80)
  Pallas kernels: 394 us -> 332 us
  local copies, waits for them, and re-layouts: 12.4 us -> 0 us
    pallas_call x3 -> x2, Pallas kernels: 234 us -> 178 us  [the longest x1 170 us: backward(): pl.pallas_call(functools.partial(backward_kernel, n, sizes, (length, keys...]
    unnamed x21 -> x0, local copies, waits for them, and re-layouts: 8.81 us -> none
    pallas_call x1, Pallas kernels: 160 us -> 154 us  [forward(): pl.pallas_call(functools.partial(forward_kernel, n, (length, keys)), name...]
where the time goes in v2:
time: 333 us
  Pallas kernels  332 us (100%)
    pallas_call x1, Pallas kernels, backward(): pl.pallas_call(functools.partial(backward_kernel, n, sizes, (length, keys...  170 us
    pallas_call x1, Pallas kernels, forward(): pl.pallas_call(functools.partial(forward_kernel, n, (length, keys)), name...  154 us
    pallas_call x1, Pallas kernels, finish(): pl.pallas_call(functools.partial(finish_kernel, sizes, len(passed), shape...  8.16 us

profile of v2, /device:TPU:0, one launch (start us, length us, event | category | flops | bytes accessed | tf_op | source)
XLA Modules:
  0.0 333.1 jit_solution(474297355053783007)
XLA Ops:
  0.7 153.9 %gather_forward.1 = (bf16[8,1024,1024]{2,1,0:T(8,128)(2,1)}, bf16[256,1024]{1,0:T(8,128)(2,1)}, bf16[4,1024,256]{2,1,0:T(8,128)(2,1)}, bf16[1024,512]{1,0:T(8,12...) custom-call(bf16[64,1024]{1,0:T(8,128)(2,1)} %refs_0_.1, ...), custom_call_target="tpu_custom_call" | custom-call | tf_op jit(solution)/shard_map/gather_forward/pallas_call | solution.py:498
  154.6 170.2 %backward_reduce.1 = (bf16[2,64,1024]{2,1,0:T(8,128)(2,1)}, bf16[2,64,512]{2,1,0:T(8,128)(2,1)}, bf16[4,64,1024]{2,1,0:T(8,128)(2,1)}, bf16[4,64,512]{2,1,0:T(8,...) custom-call(bf16[1024,256]{1,0:T(8,128)(2,1)} %get-tuple-element.67., ...), custom_call_target="tpu_custom_call" | custom-call | tf_op jit(solution)/shard_map/backward_reduce/pallas_call | solution.py:907
  324.8 8.2 %finish.1 = (f32[64,1024]{1,0:T(8,128)}, f32[64,1024]{1,0:T(8,128)}, f32[64,1024]{1,0:T(8,128)}, f32[64,1024]{1,0:T(8,128)}, f32[64,1024]{1,0:T(8,128)}, /*index...) custom-call(bf16[2,64,1024]{2,1,0:T(8,128)(2,1)} %get-tuple-element., ...), custom_call_target="tpu_custom_call" | custom-call | tf_op jit(solution)/shard_map/finish/pallas_call | solution.py:977

commit v3 on v2

--- a/solution.py
+++ b/solution.py
@@ -347,14 +347,15 @@
 
     def attention_pieces(way, r):
         c = pl.ds(way * half, half)
-        found = [lambda s: w.at[r, block(s), c], lambda s: w.at[4 + r, block(s), c],
-                 lambda s: w.at[pl.ds(2, 2), block(s), c], lambda s: w.at[pl.ds(6, 2), block(s), c]]
+        near, far = pl.ds(way * half, half // 2), pl.ds(way * half + half // 2, half // 2)
+        found = [lambda s: w.at[r, block(s), c], lambda s: w.at[4 + r, block(s), c], lambda s: w.at[2 + r, block(s), near],
+                 lambda s: w.at[pl.ds(2, 2), block(s), far], lambda s: w.at[pl.ds(6, 2), block(s), c]]
         return found + [lambda s: gn.at[s]] if way == 0 else found
 
     def feed_pieces(way, r):
         return [lambda s: gu.at[r, block(s), pl.ds(way * half_g, half_g)], lambda s: dn.at[block_d(s), pl.ds(way * half, half)]]
 
-    first = Gather(geo, attention_pieces, 2, first_sems)
+    first = Gather(geo, attention_pieces, 3, first_sems)
     second = Gather(geo, feed_pieces, 1, second_sems)
 
     width = w.shape[2]
@@ -370,7 +371,7 @@
     spot = lax.broadcasted_iota(jnp.int32, (rows, 128), 0)
     place = (lane == spot + lax.rem(me, per) * rows).astype(F32).astype(BF)
     gn[me] = jnp.concatenate([dot(g[...], place) for g in own_gains] + [jnp.zeros((5, 128), F32)], axis=0)
-    for c in loads:
+    for c in loads[:8]:
         c.wait()
     pl.semaphore_wait(barrier, 4)
 
@@ -386,6 +387,8 @@
         first.hop(t)
         first.relay(t - 1)
     lax.fori_loop(1, hops - 1, lambda t, c: (middle(t), c)[1], 0)
+    for c in loads[8:]:
+        c.wait()
     second.start()
     first.hop(hops - 1, True)
     first.relay(hops - 2)
@@ -505,7 +508,7 @@
             v(8, width, width), v(2, width, ff), v(ff, width), v(n, 8, 128, t=F32), v(table.shape[0], length, t=F32),
             v(pairs, 2 * length, length, t=F32), v(count, length, length, t=F32), v(count, length, keys, t=F32),
             v(tokens, width), v(tokens, ff), v(tokens, width, t=F32), v(tokens, width, t=F32), v(tokens, width),
-        ] + gather_sems(hops, 5, 2) + gather_sems(hops, 2, 1) + [pltpu.SemaphoreType.DMA((11,)), pltpu.SemaphoreType.DMA((16,))],
+        ] + gather_sems(hops, 6, 3) + gather_sems(hops, 2, 1) + [pltpu.SemaphoreType.DMA((11,)), pltpu.SemaphoreType.DMA((16,))],
         compiler_params=pltpu.CompilerParams(collective_id=0, has_side_effects=True, vmem_limit_bytes=67043328),
     )(*weights, *own_gains, x, enc, cot, drow, erow, buckets, table)
 
@@ -526,8 +529,9 @@
 
     def v(*shape):
         return pltpu.VMEM(shape, BF)
-    return [v(2, 2, count, rows, half), v(sib_slots, 2, count, rows, half), v(2, 2, count, rows, share), v(y_slots, 2, count, rows, share),
-            v(2, 2, count, rows, half - share), v(ring_slots, 2, count, rows, half - share)]
+    crossing = [v(2, 2, count, rows, share), v(y_slots, 2, count, rows, share)] if share else [v(16, 128), v(16, 128)]
+    return [v(2, 2, count, rows, half), v(sib_slots, 2, count, rows, half)] + crossing + [
+        v(2, 2, count, rows, half - share), v(ring_slots, 2, count, rows, half - share)]
 
 
 def reduce_sems(groups, slots):
@@ -542,6 +546,7 @@
     def __init__(self, geo, groups, slots, sems):
         self.chips, self.me, self.rep, self.core, self.ring, self.device_at = geo
         self.groups = groups
+        self.shared = groups[0].share > 0
         self.slots = slots
         self.sib_s, self.sib_r, self.y_s, self.y_r, self.ring_s, self.ring_r, self.fin_s, self.fin_r, self.free = sems
         self.other = 1 - self.rep
@@ -623,26 +628,35 @@
                 c.start()
         each(2, go)
 
-    def to_ring(self, t):
+    def to_ring(self, t, at_once):
         s, b, y, r = lax.rem(t, 2), lax.rem(t, self.slots[0]), lax.rem(t, self.slots[1]), lax.rem(t, self.slots[2])
 
         for k, g in enumerate(self.groups):
             def go(way, k=k, g=g):
                 dev = self.block(t, way, self.core)
+                if not self.shared:
+                    self.sib_copies(t, way)[k].wait_recv()
+                lo, wide = 2 * g.share, g.half - 2 * g.share
+                at = pl.multiple_of(self.rep * g.share, 128)
+                common, apart = [], []
+                for i in range(g.count):
+                    if self.shared:
+                        v = g.part(i, dev, way * g.half + at, g.share)
+                        common.append(v + g.sr[b, way, i, :, pl.ds(at, g.share)].astype(F32))
+                    v = g.part(i, dev, way * g.half + lo, wide)
+                    apart.append(v + g.sr[b, way, i, :, lo:].astype(F32))
                 self.settle(t, self.ring_copies(t, way)[k:k + 1])
-                self.y_copies(t, way)[k].wait_recv()
+                if self.shared:
+                    self.y_copies(t, way)[k].wait_recv()
 
                 @pl.when(t >= 1)
                 def _():
                     self.ring_copies(t - 1, way)[k].wait_recv()
-                at = pl.multiple_of(self.rep * g.share, 128)
                 for i in range(g.count):
-                    v = g.part(i, dev, way * g.half + at, g.share) + g.sr[b, way, i, :, pl.ds(at, g.share)].astype(F32)
-                    v = v + g.yr[y, way, i].astype(F32) + g.rr[r, way, i, :, :g.share].astype(F32)
-                    g.rs[s, way, i, :, :g.share] = v.astype(BF)
-                    v = g.part(i, dev, way * g.half + 2 * g.share, g.half - 2 * g.share)
-                    v = v + g.sr[b, way, i, :, 2 * g.share:].astype(F32) + g.rr[r, way, i, :, g.share:].astype(F32)
-                    g.rs[s, way, i, :, g.share:] = v.astype(BF)
+                    if self.shared:
+                        v = common[i] + g.yr[y, way, i].astype(F32) + g.rr[r, way, i, :, :g.share].astype(F32)
+                        g.rs[s, way, i, :, :g.share] = v.astype(BF)
+                    g.rs[s, way, i, :, g.share:] = (apart[i] + g.rr[r, way, i, :, g.share:].astype(F32)).astype(BF)
 
                 @pl.when(t < self.chips - 1)
                 def _():
@@ -652,55 +666,60 @@
 
                 @pl.when(t == self.chips - 1)
                 def _():
-                    for c in self.final_copies(way, k):
-                        c.start()
+                    if at_once:
+                        self.send_final(way, k)
                     last = (self.chips - 1) % 2
-                    cols = pl.ds(pl.multiple_of(way * g.half + self.rep * g.share, 128), g.share)
-                    g.own[:, :, cols] = g.rs[last, way, :, :, :g.share]
-                    rest = pl.ds(pl.multiple_of(way * g.half + 2 * g.share, 128), g.half - 2 * g.share)
+                    if self.shared:
+                        cols = pl.ds(pl.multiple_of(way * g.half + self.rep * g.share, 128), g.share)
+                        g.own[:, :, cols] = g.rs[last, way, :, :, :g.share]
+                    rest = pl.ds(pl.multiple_of(way * g.half + lo, 128), wide)
                     g.own[:, :, rest] = g.rs[last, way, :, :, g.share:]
                 if k == len(self.groups) - 1:
                     self.release(0, t, way, self.sibling)
-                    self.release(1, t, way, self.opposite)
+                    if self.shared:
+                        self.release(1, t, way, self.opposite)
                     self.release(2, t, way, self.behind(way))
             each(2, go)
 
-    def prepare(self):
-        for g in self.groups:
-            g.rr[0] = jnp.zeros(g.rr.shape[1:], BF)
+    def send_final(self, way, k):
+        for c in self.final_copies(way, k):
+            c.start()
 
     def final_copies(self, way, k):
         g = self.groups[k]
         mine = g.rs.at[(self.chips - 1) % 2, way]
-        cols = pl.ds(pl.multiple_of(way * g.half + self.rep * g.share, 128), g.share)
+        cols = pl.ds(pl.multiple_of(way * g.half + self.rep * g.share, 128), g.share) if g.share else None
         wide = g.half - 2 * g.share
         there = pl.ds(pl.multiple_of(way * wide, 128), wide)
-        return [rdma(mine.at[:, :, pl.ds(0, g.share)], g.own.at[:, :, cols],
-                     self.fin_s.at[way, 2 * k], self.fin_r.at[way, 2 * k], self.opposite),
-                rdma(mine.at[:, :, pl.ds(g.share, wide)], g.got.at[:, :, there],
-                     self.fin_s.at[way, 2 * k + 1], self.fin_r.at[way, 2 * k + 1], self.opposite)]
+        found = [rdma(mine.at[:, :, pl.ds(g.share, wide)], g.got.at[:, :, there],
+                      self.fin_s.at[way, 2 * k + 1], self.fin_r.at[way, 2 * k + 1], self.opposite)]
+        if self.shared:
+            found.append(rdma(mine.at[:, :, pl.ds(0, g.share)], g.own.at[:, :, cols],
+                              self.fin_s.at[way, 2 * k], self.fin_r.at[way, 2 * k], self.opposite))
+        return found
 
     def finish(self):
         def go(way):
             for k, g in enumerate(self.groups):
                 wide = g.half - 2 * g.share
-                ref = g.own.at[:, :, pl.ds(pl.multiple_of(way * g.half + self.other * g.share, 128), g.share)]
-                rdma(ref, ref, self.fin_s.at[way, 2 * k], self.fin_r.at[way, 2 * k], self.opposite).wait_recv()
+                if self.shared:
+                    ref = g.own.at[:, :, pl.ds(pl.multiple_of(way * g.half + self.other * g.share, 128), g.share)]
+                    rdma(ref, ref, self.fin_s.at[way, 2 * k], self.fin_r.at[way, 2 * k], self.opposite).wait_recv()
                 ref = g.got.at[:, :, pl.ds(pl.multiple_of(way * wide, 128), wide)]
                 rdma(ref, ref, self.fin_s.at[way, 2 * k + 1], self.fin_r.at[way, 2 * k + 1], self.opposite).wait_recv()
                 for c in self.final_copies(way, k):
                     c.wait_send()
             for t in (self.chips - 2, self.chips - 1):
-                for c in self.sib_copies(t, way) + self.y_copies(t, way):
+                for c in self.sib_copies(t, way) + (self.y_copies(t, way) if self.shared else []):
                     c.wait_send()
             for c in self.ring_copies(self.chips - 2, way):
                 c.wait_send()
         each(2, go)
 
-    def at(self, t, f):
+    def at(self, t, f, *more):
         @pl.when((t >= 0) & (t < self.chips))
         def _():
-            f(t)
+            f(t, *more)
 
 
 class Butterfly:
@@ -732,17 +751,19 @@
 
 
 OFFSETS = (0, 0, 0, 5, 8)
-CHAINS = ((2,), (3,), (4,), (0, 5), (1,))
+FINALS = (1, 2, 3, 1, 0)
+CHAINS = ((2,), (3,), (4,), (0, 5), (1, 6))
 SLOTS = (3, 3, 3)
+FIRST_PIECE = 0
 
 
 def backward_kernel(n, sizes, dims, *refs):
     length, keys = dims
     ins, w_hbm, refs = refs[:16], refs[16], refs[17:]
-    outs, (small_o, dtok, denc), refs = refs[:12], refs[12:15], refs[15:]
+    outs, (small_o, dtok, denc), refs = refs[:14], refs[14:17], refs[17:]
     held, refs = refs[:16], refs[16:]
     hfft, hidt, dgu, cot, r1, cq, ckv, p2, x1, gains, qkv, p1, x, xt, enct, gain3 = held
-    bufs, refs = refs[:36], refs[36:]
+    bufs, refs = refs[:42], refs[42:]
     sems, refs = [refs[9 * k:9 * k + 9] for k in range(5)], refs[45:]
     sm, sm_got, sm_s, sm_r, load_s, w, w_s, dy, dye, dh, r0, do, gain12, diag = refs
     geo = geometry(n)
@@ -750,22 +771,20 @@
     rows, rows_d = sizes[0][1], sizes[4][1]
 
     loads = [pltpu.make_async_copy(a, b, load_s.at[i]) for i, (a, b) in enumerate(zip(ins, held))]
-    for c in loads:
+    for c in loads[:4]:
         c.start()
 
     def fetch(i, slot):
         return pltpu.make_async_copy(w_hbm.at[i], w.at[slot], w_s.at[slot])
-    for i, slot in ((5, 0), (6, 1), (7, 2), (4, 3)):
-        fetch(i, slot).start()
 
     def block(dev, size):
         return pl.ds(pl.multiple_of(dev * size, size), size)
-    lefts = [lambda i, dev: xt[(3, 2)[i], block(dev, rows), :], lambda i, dev: xt[(1, 0, 0, 0)[i], block(dev, rows), :],
+    lefts = [lambda i, dev: xt[(3, 2)[i], block(dev, rows), :], lambda i, dev: xt[(1, 0)[i], block(dev, rows), :],
              lambda i, dev: hfft[block(dev, rows), :], lambda i, dev: hfft[block(dev, rows), :],
-             lambda i, dev: hidt[block(dev, rows_d), :], lambda i, dev: enct[block(dev, rows), :]]
+             lambda i, dev: hidt[block(dev, rows_d), :], lambda i, dev: enct[block(dev, rows), :], lambda i, dev: xt[0, block(dev, rows), :]]
     rights = [lambda i, c: dy[i, :, c], lambda i, c: dy[2 + i, :, c], lambda i, c: dgu[0, :, c], lambda i, c: dgu[1, :, c],
-              lambda i, c: cot[:, c], lambda i, c: dye[i, :, c]]
-    groups = [Group(lefts[k], rights[k], sizes[k], bufs[6 * k:6 * k + 6] + outs[2 * k:2 * k + 2]) for k in range(6)]
+              lambda i, c: cot[:, c], lambda i, c: dye[i, :, c], lambda i, c: dy[4 + i, :, c]]
+    groups = [Group(lefts[k], rights[k], sizes[k], bufs[6 * k:6 * k + 6] + outs[2 * k:2 * k + 2]) for k in range(7)]
     chains = [Reduce(geo, [groups[k] for k in c], SLOTS, s) for c, s in zip(CHAINS, sems)]
     tree = Butterfly(geo, n, sm, sm_got, (sm_s, sm_r))
     lead = chains[0]
@@ -779,6 +798,10 @@
     diag[...] = jnp.zeros(diag.shape, F32)
     for c in loads[:4]:
         c.wait()
+    for c in loads[4:]:
+        c.start()
+    for i, slot in ((5, 0), (6, 1), (7, 2), (4, 3)):
+        fetch(i, slot).start()
     pl.semaphore_wait(barrier, len(greet))
 
     total = p1.shape[0]
@@ -855,16 +878,22 @@
 
     def piece(u, which):
         for i in range(which, len(pieces), 3):
-            pl.when(u == i // 3)(pieces[i])
+            pl.when(u == i // 3 + FIRST_PIECE)(pieces[i])
 
     def step(v, bit):
         u = v - 3
         for k, c in enumerate(chains):
-            c.at(u - OFFSETS[k], c.to_ring)
+            t = u - OFFSETS[k]
+            c.at(t, c.to_ring, FINALS[k] == 0)
             if k < 3:
                 piece(u, k)
+            if FINALS[k]:
+                for way in range(2):
+                    for j in range(len(c.groups)):
+                        pl.when(t == chips - 1 + FINALS[k] + way)(functools.partial(c.send_final, way, j))
         for k, c in enumerate(chains):
-            c.at(u - OFFSETS[k] + 2, c.to_across)
+            if c.shared:
+                c.at(u - OFFSETS[k] + 2, c.to_across)
         for k, c in enumerate(chains):
             c.at(u - OFFSETS[k] + 3, c.to_sibling)
         pl.when(u == tree_at)(tree.begin)
@@ -881,8 +910,8 @@
         c.finish()
 
 
-def shares(half):
-    return max(1, half // 512) * 128
+def shares(half, part):
+    return half * part // 1408 * 128
 
 
 def backward(n, w, hfft, hidt, dgu, cot, r1, cq, ckv, p2, x1, gains, qkv, p1, x, xt, enct, gain3):
@@ -892,8 +921,9 @@
     length, keys = p1.shape[2], p2.shape[2]
     rows, rows_d = width // n, hidt.shape[0] // n
     half, half_g = width // 2, ff // 2
-    sizes = [(2, rows, half, shares(half)), (4, rows, half, shares(half)), (1, rows, half_g, shares(half_g)),
-             (1, rows, half_g, shares(half_g)), (1, rows_d, half, shares(half)), (2, rows, half, shares(half))]
+    part = shares(half, 3)
+    sizes = [(2, rows, half, part), (2, rows, half, part), (1, rows, half_g, shares(half_g, 3)),
+             (1, rows, half_g, shares(half_g, 3)), (1, rows_d, half, part), (2, rows, half, part), (2, rows, half, part)]
     stages = n.bit_length() - 1
     dma = pltpu.SemaphoreType.DMA
     S = jax.ShapeDtypeStruct
@@ -909,7 +939,7 @@
         name="backward_reduce",
         out_shape=tuple(outs) + (S(small, F32), S((tokens, width), F32), S((etokens, width), F32)),
         in_specs=[hbm] * 17,
-        out_specs=[vm] * 15,
+        out_specs=[vm] * 17,
         scratch_shapes=[pltpu.VMEM(a.shape, a.dtype) for a in ins]
         + [b for size in sizes for b in group_shapes(size, slots)]
         + [s for c in CHAINS for s in reduce_sems(len(c), slots)]
@@ -939,7 +969,8 @@
         for i in range(count):
             for way in range(2):
                 lo = way * half
-                done[at][:, lo:lo + 2 * share] = own[i, :, lo:lo + 2 * share].astype(F32)
+                if share:
+                    done[at][:, lo:lo + 2 * share] = own[i, :, lo:lo + 2 * share].astype(F32)
                 v = own[i, :, lo + 2 * share:lo + half].astype(F32) + got[i, :, way * wide:(way + 1) * wide].astype(F32)
                 done[at][:, lo + 2 * share:lo + half] = v
             stores[at].start()
@@ -1005,7 +1036,7 @@
     w, out, xt, enct, hfft, hidt, dgu, r1, x1, qkv, cq, ckv, p1, p2, gain3, gains = forward(
         n, weights, own_gains, x, enc, cot, dec_segments.reshape(count, 1, length), enc_segments.reshape(count, 1, keys), buckets, table.T)
     *parts, small, dtok, denc = backward(n, w, hfft, hidt, dgu, cot, r1, cq, ckv, p2, x1, gains, qkv, p1, x, xt, enct, gain3)
-    gco, gcq, gso, gq, gk, gv, gg, gup, gd, gck, gcv, out, dtok, denc, dtable, g1, g2, g3 = finish(
+    gco, gcq, gso, gq, gg, gup, gd, gck, gcv, gk, gv, out, dtok, denc, dtable, g1, g2, g3 = finish(
         parts, (out, dtok, denc), small, buckets, table.T.shape, rows)
     if spare:
         gd = gd[:rows_d]

time: 333 us -> 323 us (0.970)
  Pallas kernels: 332 us -> 322 us
    pallas_call x1, Pallas kernels: 170 us -> 164 us  [backward(): pl.pallas_call(functools.partial(backward_kernel, n, sizes, (length, keys...]
    pallas_call x1, Pallas kernels: 154 us -> 150 us  [forward(): pl.pallas_call(functools.partial(forward_kernel, n, (length, keys)), name...]
where the time goes in v3:
time: 323 us
  Pallas kernels  322 us (100%)
    pallas_call x1, Pallas kernels, backward(): pl.pallas_call(functools.partial(backward_kernel, n, sizes, (length, keys...  164 us
    pallas_call x1, Pallas kernels, forward(): pl.pallas_call(functools.partial(forward_kernel, n, (length, keys)), name...  150 us
    pallas_call x1, Pallas kernels, finish(): pl.pallas_call(functools.partial(finish_kernel, sizes, len(passed), shape...  8.15 us

profile of v3, /device:TPU:0, one launch (start us, length us, event | category | flops | bytes accessed | tf_op | source)
XLA Modules:
  0.0 322.7 jit_solution(9061193776330766408)
XLA Ops:
  0.7 150.1 %gather_forward.1 = (bf16[8,1024,1024]{2,1,0:T(8,128)(2,1)}, bf16[256,1024]{1,0:T(8,128)(2,1)}, bf16[4,1024,256]{2,1,0:T(8,128)(2,1)}, bf16[1024,512]{1,0:T(8,12...) custom-call(bf16[64,1024]{1,0:T(8,128)(2,1)} %refs_0_.1, ...), custom_call_target="tpu_custom_call" | custom-call | tf_op jit(solution)/shard_map/gather_forward/pallas_call | solution.py:501
  150.8 163.7 %backward_reduce.1 = (bf16[2,64,1024]{2,1,0:T(8,128)(2,1)}, bf16[2,64,512]{2,1,0:T(8,128)(2,1)}, bf16[2,64,1024]{2,1,0:T(8,128)(2,1)}, bf16[2,64,512]{2,1,0:T(8,...) custom-call(bf16[1024,256]{1,0:T(8,128)(2,1)} %get-tuple-element.69., ...), custom_call_target="tpu_custom_call" | custom-call | tf_op jit(solution)/shard_map/backward_reduce/pallas_call | solution.py:937
  314.4 8.1 %finish.1 = (f32[64,1024]{1,0:T(8,128)}, f32[64,1024]{1,0:T(8,128)}, f32[64,1024]{1,0:T(8,128)}, f32[64,1024]{1,0:T(8,128)}, f32[64,2816]{1,0:T(8,128)}, /*index...) custom-call(bf16[2,64,1024]{2,1,0:T(8,128)(2,1)} %get-tuple-element., ...), custom_call_target="tpu_custom_call" | custom-call | tf_op jit(solution)/shard_map/finish/pallas_call | solution.py:1008

commit v4 on v3

--- a/solution.py
+++ b/solution.py
@@ -268,8 +268,10 @@
         for c in self.own_copies(self.me):
             c.start()
 
-    def hop(self, t, last=False):
+    def hop(self, t, last=False, which=None):
         for way, p, ref in self.each(self.rep):
+            if which is not None and p != which:
+                continue
             r = ref(self.source(way, t))
             self.ring_copy(way, t, p, r).wait_recv()
             if not last:
@@ -409,25 +411,29 @@
 
     def heads():
         normed(x, gains.at[0], h)
-        for i in range(3):
+        project(h, w.at[0], qkv.at[0])
+
+    def keys_values():
+        for i in range(1, 3):
             project(h, w.at[i], qkv.at[i])
 
     def own(i):
         attend(i, qkv.at[0], qkv.at[1], qkv.at[2], p1, o, neg_s, bias, length, length)
 
-    def cross_heads():
+    def own_result():
         store(8, 11)
         turn(h, xt.at[0])
         turn(o, xt.at[1])
         project(o, w.at[3], x1, base=x, kind=F32)
+
+    def cross_heads():
         normed(x1, gains.at[1], h)
         project(h, w.at[4], cq)
 
     def cross_keys():
         store(7, 9)
         turn(h, xt.at[2])
-        for i in range(2):
-            project(enc, w.at[6 + i], ckv.at[i])
+        project(enc, w.at[6], ckv.at[0])
 
     def cross(i):
         attend(i, cq, ckv.at[0], ckv.at[1], p2, o, neg_c, None, length, keys)
@@ -442,14 +448,17 @@
         store(3)
 
     total = count * pairs
-    mid = total // 2
-    chunks = [heads, lambda: some(0, mid, own), lambda: some(mid, total, own), cross_heads, cross_keys,
-              lambda: some(0, mid, cross), lambda: some(mid, total, cross)]
+    def quarters(f):
+        return [functools.partial(some, total * k // 4, total * (k + 1) // 4, f) for k in range(4)]
+    halves = [heads, keys_values] + quarters(own) + [own_result, cross_heads, cross_keys, lambda: project(enc, w.at[7], ckv.at[1])] + quarters(cross)
+    chunks = list(zip(halves[0::2], halves[1::2]))
     for t in range(len(chunks)):
-        chunks[t]()
-        second.hop(t, t == hops - 1)
+        chunks[t][0]()
+        second.hop(t, t == hops - 1, 0)
         if t > 0:
             second.relay(t - 1)
+        chunks[t][1]()
+        second.hop(t, t == hops - 1, 1)
     if hops > len(chunks):
         def rest(t):
             second.hop(t)
@@ -751,7 +760,7 @@
 
 
 OFFSETS = (0, 0, 0, 5, 8)
-FINALS = (1, 2, 3, 1, 0)
+FINALS = (0, 1, 2, 0, 0)
 CHAINS = ((2,), (3,), (4,), (0, 5), (1, 6))
 SLOTS = (3, 3, 3)
 FIRST_PIECE = 0
@@ -760,12 +769,14 @@
 def backward_kernel(n, sizes, dims, *refs):
     length, keys = dims
     ins, w_hbm, refs = refs[:16], refs[16], refs[17:]
-    outs, (small_o, dtok, denc), refs = refs[:14], refs[14:17], refs[17:]
+    kept, (small_o,), refs = refs[:16], refs[16:17], refs[17:]
+    done, refs = refs[:16], refs[16:]
+    outs, (dtok, denc) = done[:14], done[14:]
     held, refs = refs[:16], refs[16:]
     hfft, hidt, dgu, cot, r1, cq, ckv, p2, x1, gains, qkv, p1, x, xt, enct, gain3 = held
     bufs, refs = refs[:42], refs[42:]
     sems, refs = [refs[9 * k:9 * k + 9] for k in range(5)], refs[45:]
-    sm, sm_got, sm_s, sm_r, load_s, w, w_s, dy, dye, dh, r0, do, gain12, diag = refs
+    sm, sm_got, sm_s, sm_r, load_s, w, w_s, dy, dye, dh, r0, do, gain12, diag, store_s = refs
     geo = geometry(n)
     chips, me, rep, core, ring, device_at = geo
     rows, rows_d = sizes[0][1], sizes[4][1]
@@ -773,6 +784,9 @@
     loads = [pltpu.make_async_copy(a, b, load_s.at[i]) for i, (a, b) in enumerate(zip(ins, held))]
     for c in loads[:4]:
         c.start()
+
+    def stored(i):
+        return pltpu.make_async_copy(done[i], kept[i], store_s.at[i])
 
     def fetch(i, slot):
         return pltpu.make_async_copy(w_hbm.at[i], w.at[slot], w_s.at[slot])
@@ -834,6 +848,7 @@
                 fetch(7, 2).wait()
             project_t([(dye.at[0], w.at[1]), (dye.at[1], w.at[2])], denc, begin=begin, end=end)
             if last:
+                stored(15).start()
                 fetch(0, 1).start()
                 fetch(1, 2).start()
         return f
@@ -861,6 +876,7 @@
 
     def own_norm():
         norm_back(x, gains.at[0], dh, r0, dtok, gain12.at[0])
+        stored(14).start()
         for k in range(width // 128):
             for i, g in enumerate((gain12.at[0], gain12.at[1], gain3)):
                 sm[0, pl.ds(i * (width // 128) + k, 1), :] = g[:, k * 128:(k + 1) * 128]
@@ -906,8 +922,13 @@
 
     lax.fori_loop(0, OFFSETS[-1] + chips + 3, step, jnp.int32(1))
     tree.end(small_o)
-    for c in chains:
+    for k, c in enumerate(chains):
         c.finish()
+        for g in CHAINS[k]:
+            stored(2 * g).start()
+            stored(2 * g + 1).start()
+    for i in range(16):
+        stored(i).wait()
 
 
 def shares(half, part):
@@ -931,22 +952,24 @@
     outs = []
     for count, r, h, share in sizes:
         outs += [S((count, r, 2 * h), BF), S((count, r, 2 * (h - 2 * share)), BF)]
+    outs += [S((tokens, width), F32), S((etokens, width), F32)]
     small = (3 * (width // 128) + width // 64, 128)
     ins = (hfft, hidt, dgu, cot, r1, cq, ckv, p2, x1, gains, qkv, p1, x, xt, enct, gain3)
     slots = tuple(min(s, chips) for s in SLOTS)
     return pl.pallas_call(
         functools.partial(backward_kernel, n, sizes, (length, keys)),
         name="backward_reduce",
-        out_shape=tuple(outs) + (S(small, F32), S((tokens, width), F32), S((etokens, width), F32)),
+        out_shape=tuple(outs) + (S(small, F32),),
         in_specs=[hbm] * 17,
-        out_specs=[vm] * 17,
-        scratch_shapes=[pltpu.VMEM(a.shape, a.dtype) for a in ins]
+        out_specs=[hbm] * 16 + [vm],
+        scratch_shapes=[pltpu.VMEM(a.shape, a.dtype) for a in outs] + [pltpu.VMEM(a.shape, a.dtype) for a in ins]
         + [b for size in sizes for b in group_shapes(size, slots)]
         + [s for c in CHAINS for s in reduce_sems(len(c), slots)]
         + [pltpu.VMEM((stages + 1,) + small, F32)] * 2 + [dma((stages + 1,))] * 2
         + [dma((16,)), pltpu.VMEM((4, width, width), BF), dma((4,)), pltpu.VMEM((6, tokens, width), BF),
            pltpu.VMEM((2, etokens, width), BF), pltpu.VMEM((tokens, width), F32), pltpu.VMEM((tokens, width), F32),
-           pltpu.VMEM((tokens, width), BF), pltpu.VMEM((2, 1, width), F32), pltpu.VMEM((width // 64, 1, 128), F32)],
+           pltpu.VMEM((tokens, width), BF), pltpu.VMEM((2, 1, width), F32), pltpu.VMEM((width // 64, 1, 128), F32),
+           dma((16,))],
         compiler_params=pltpu.CompilerParams(collective_id=1, has_side_effects=True, vmem_limit_bytes=67043328),
     )(*ins, w)
 
@@ -1035,7 +1058,7 @@
     own_gains = [g.reshape(1, rows) for g in (norm_self, norm_cross, norm_ff)]
     w, out, xt, enct, hfft, hidt, dgu, r1, x1, qkv, cq, ckv, p1, p2, gain3, gains = forward(
         n, weights, own_gains, x, enc, cot, dec_segments.reshape(count, 1, length), enc_segments.reshape(count, 1, keys), buckets, table.T)
-    *parts, small, dtok, denc = backward(n, w, hfft, hidt, dgu, cot, r1, cq, ckv, p2, x1, gains, qkv, p1, x, xt, enct, gain3)
+    *parts, dtok, denc, small = backward(n, w, hfft, hidt, dgu, cot, r1, cq, ckv, p2, x1, gains, qkv, p1, x, xt, enct, gain3)
     gco, gcq, gso, gq, gg, gup, gd, gck, gcv, gk, gv, out, dtok, denc, dtable, g1, g2, g3 = finish(
         parts, (out, dtok, denc), small, buckets, table.T.shape, rows)
     if spare:

time: 323 us -> 318 us (0.985)
  Pallas kernels: 322 us -> 317 us
    pallas_call x1, Pallas kernels: 164 us -> 160 us  [backward(): pl.pallas_call(functools.partial(backward_kernel, n, sizes, (length, keys...]
where the time goes in v4:
time: 318 us
  Pallas kernels  317 us (100%)
    pallas_call x1, Pallas kernels, backward(): pl.pallas_call(functools.partial(backward_kernel, n, sizes, (length, keys...  160 us
    pallas_call x1, Pallas kernels, forward(): pl.pallas_call(functools.partial(forward_kernel, n, (length, keys)), name...  149 us
    pallas_call x1, Pallas kernels, finish(): pl.pallas_call(functools.partial(finish_kernel, sizes, len(passed), shape...  8.15 us

profile of v4, /device:TPU:0, one launch (start us, length us, event | category | flops | bytes accessed | tf_op | source)
XLA Modules:
  0.0 318.0 jit_solution(6076910024519738666)
XLA Ops:
  0.7 149.2 %gather_forward.1 = (bf16[8,1024,1024]{2,1,0:T(8,128)(2,1)}, bf16[256,1024]{1,0:T(8,128)(2,1)}, bf16[4,1024,256]{2,1,0:T(8,128)(2,1)}, bf16[1024,512]{1,0:T(8,12...) custom-call(bf16[64,1024]{1,0:T(8,128)(2,1)} %refs_0_.1, ...), custom_call_target="tpu_custom_call" | custom-call | tf_op jit(solution)/shard_map/gather_forward/pallas_call | solution.py:510
  149.9 159.8 %backward_reduce.1 = (bf16[2,64,1024]{2,1,0:T(8,128)(2,1)}, bf16[2,64,512]{2,1,0:T(8,128)(2,1)}, bf16[2,64,1024]{2,1,0:T(8,128)(2,1)}, bf16[2,64,512]{2,1,0:T(8,...) custom-call(bf16[1024,256]{1,0:T(8,128)(2,1)} %get-tuple-element.69., ...), custom_call_target="tpu_custom_call" | custom-call | tf_op jit(solution)/shard_map/backward_reduce/pallas_call | solution.py:959
  309.7 8.1 %finish.1 = (f32[64,1024]{1,0:T(8,128)}, f32[64,1024]{1,0:T(8,128)}, f32[64,1024]{1,0:T(8,128)}, f32[64,1024]{1,0:T(8,128)}, f32[64,2816]{1,0:T(8,128)}, /*index...) custom-call(bf16[2,64,1024]{2,1,0:T(8,128)(2,1)} %get-tuple-element., ...), custom_call_target="tpu_custom_call" | custom-call | tf_op jit(solution)/shard_map/finish/pallas_call | solution.py:1031

commit v5 on v4

--- a/solution.py
+++ b/solution.py
@@ -810,12 +810,12 @@
     for g in groups:
         g.rr[0] = jnp.zeros(g.rr.shape[1:], BF)
     diag[...] = jnp.zeros(diag.shape, F32)
-    for c in loads[:4]:
-        c.wait()
     for c in loads[4:]:
         c.start()
     for i, slot in ((5, 0), (6, 1), (7, 2), (4, 3)):
         fetch(i, slot).start()
+    for c in loads[:4]:
+        c.wait()
     pl.semaphore_wait(barrier, len(greet))
 
     total = p1.shape[0]
@@ -981,10 +981,14 @@
     held, done, (load_s, store_s) = refs[:parts + passed], refs[parts + passed:-2], refs[-2:]
     loads = [pltpu.make_async_copy(a, b, load_s.at[i]) for i, (a, b) in enumerate(zip(ins, held))]
     stores = [pltpu.make_async_copy(a, b, store_s.at[i]) for i, (a, b) in enumerate(zip(done + held[parts:], outs))]
-    for c in loads:
+    for c in loads[:2] + loads[parts:] + loads[2:parts]:
         c.start()
     at = 0
     for k, (count, rows, half, share) in enumerate(sizes):
+        if k == 1:
+            for i in range(passed):
+                loads[parts + i].wait()
+                stores[mats + i].start()
         own, got = held[2 * k], held[2 * k + 1]
         loads[2 * k].wait()
         loads[2 * k + 1].wait()
@@ -998,9 +1002,6 @@
                 done[at][:, lo + 2 * share:lo + half] = v
             stores[at].start()
             at += 1
-    for i in range(passed):
-        loads[parts + i].wait()
-        stores[mats + i].start()
     me = lax.axis_index("shard")
     rows = gain1.shape[1]
     per = 128 // rows

time: 318 us -> 317 us (level)
  no operation moved by 1% of the time
where the time goes in v5:
time: 317 us; the launch traced here: 316 us
  Pallas kernels  316 us (100%)
    pallas_call x1, Pallas kernels, backward(): pl.pallas_call(functools.partial(backward_kernel, n, sizes, (length, keys...  159 us
    pallas_call x1, Pallas kernels, forward(): pl.pallas_call(functools.partial(forward_kernel, n, (length, keys)), name...  149 us
    pallas_call x1, Pallas kernels, finish(): pl.pallas_call(functools.partial(finish_kernel, sizes, len(passed), shape...  6.99 us

profile of v5, /device:TPU:0, one launch (start us, length us, event | category | flops | bytes accessed | tf_op | source)
XLA Modules:
  0.0 316.4 jit_solution(14189620063382312814)
XLA Ops:
  0.7 149.2 %gather_forward.1 = (bf16[8,1024,1024]{2,1,0:T(8,128)(2,1)}, bf16[256,1024]{1,0:T(8,128)(2,1)}, bf16[4,1024,256]{2,1,0:T(8,128)(2,1)}, bf16[1024,512]{1,0:T(8,12...) custom-call(bf16[64,1024]{1,0:T(8,128)(2,1)} %refs_0_.1, ...), custom_call_target="tpu_custom_call" | custom-call | tf_op jit(solution)/shard_map/gather_forward/pallas_call | solution.py:510
  149.9 159.4 %backward_reduce.1 = (bf16[2,64,1024]{2,1,0:T(8,128)(2,1)}, bf16[2,64,512]{2,1,0:T(8,128)(2,1)}, bf16[2,64,1024]{2,1,0:T(8,128)(2,1)}, bf16[2,64,512]{2,1,0:T(8,...) custom-call(bf16[1024,256]{1,0:T(8,128)(2,1)} %get-tuple-element.69., ...), custom_call_target="tpu_custom_call" | custom-call | tf_op jit(solution)/shard_map/backward_reduce/pallas_call | solution.py:959
  309.3 7.0 %finish.1 = (f32[64,1024]{1,0:T(8,128)}, f32[64,1024]{1,0:T(8,128)}, f32[64,1024]{1,0:T(8,128)}, f32[64,1024]{1,0:T(8,128)}, f32[64,2816]{1,0:T(8,128)}, /*index...) custom-call(bf16[2,64,1024]{2,1,0:T(8,128)(2,1)} %get-tuple-element., ...), custom_call_target="tpu_custom_call" | custom-call | tf_op jit(solution)/shard_map/finish/pallas_call | solution.py:1032

commit v6 on v5

--- a/solution.py
+++ b/solution.py
@@ -759,7 +759,7 @@
             self.copy(j, self.partner(1)).wait_send()
 
 
-OFFSETS = (0, 0, 0, 5, 8)
+OFFSETS = (0, 0, 0, 6, 8)
 FINALS = (0, 1, 2, 0, 0)
 CHAINS = ((2,), (3,), (4,), (0, 5), (1, 6))
 SLOTS = (3, 3, 3)

time: 317 us -> 316 us (level)
  no operation moved by 1% of the time
where the time goes in v6:
time: 316 us; the launch traced here: 315 us
  Pallas kernels  315 us (100%)
    pallas_call x1, Pallas kernels, backward(): pl.pallas_call(functools.partial(backward_kernel, n, sizes, (length, keys...  158 us
    pallas_call x1, Pallas kernels, forward(): pl.pallas_call(functools.partial(forward_kernel, n, (length, keys)), name...  149 us
    pallas_call x1, Pallas kernels, finish(): pl.pallas_call(functools.partial(finish_kernel, sizes, len(passed), shape...  6.99 us

profile of v6, /device:TPU:0, one launch (start us, length us, event | category | flops | bytes accessed | tf_op | source)
XLA Modules:
  0.0 315.4 jit_solution(7327935020957930076)
XLA Ops:
  0.7 149.2 %gather_forward.1 = (bf16[8,1024,1024]{2,1,0:T(8,128)(2,1)}, bf16[256,1024]{1,0:T(8,128)(2,1)}, bf16[4,1024,256]{2,1,0:T(8,128)(2,1)}, bf16[1024,512]{1,0:T(8,12...) custom-call(bf16[64,1024]{1,0:T(8,128)(2,1)} %refs_0_.1, ...), custom_call_target="tpu_custom_call" | custom-call | tf_op jit(solution)/shard_map/gather_forward/pallas_call | solution.py:510
  149.9 158.4 %backward_reduce.1 = (bf16[2,64,1024]{2,1,0:T(8,128)(2,1)}, bf16[2,64,512]{2,1,0:T(8,128)(2,1)}, bf16[2,64,1024]{2,1,0:T(8,128)(2,1)}, bf16[2,64,512]{2,1,0:T(8,...) custom-call(bf16[1024,256]{1,0:T(8,128)(2,1)} %get-tuple-element.69., ...), custom_call_target="tpu_custom_call" | custom-call | tf_op jit(solution)/shard_map/backward_reduce/pallas_call | solution.py:959
  308.3 7.0 %finish.1 = (f32[64,1024]{1,0:T(8,128)}, f32[64,1024]{1,0:T(8,128)}, f32[64,1024]{1,0:T(8,128)}, f32[64,1024]{1,0:T(8,128)}, f32[64,2816]{1,0:T(8,128)}, /*index...) custom-call(bf16[2,64,1024]{2,1,0:T(8,128)(2,1)} %get-tuple-element., ...), custom_call_target="tpu_custom_call" | custom-call | tf_op jit(solution)/shard_map/finish/pallas_call | solution.py:1032
